TPU v7x, 128 devices: a whole 4x4x4 slice. The times are simulated.
128 devices in a mesh: lat: 4 (over x_lo, core), lon: 32 (over x_hi, y, z).
Axes of the slice: x: 4 (x_hi: 2, x_lo: 2; x = x_hi * 2 + x_lo), y: 4, z: 4, core: 2. Of those that a mesh axis runs over, the one named last changes fastest.
Arguments:
- air_temp: float32 [128, 2880, 128], P('lat', 'lon'), may hold values from -6 to 6
- sea_temp: float32 [128, 2880], P(('lat', 'lon')), may hold values from -6 to 6
- land_sea: int32 [128, 2880], P('lat', 'lon'), may hold values 0 or 1
- courant: float32 [128], replicated, may hold values from -0.4 to 0.4
- vertical_mix: float32 [128, 128], replicated, may hold values from -0.25 to 0.25
- cutoffs: int32 [32], replicated, may hold values from 1 to 127, as said below
Outputs:
- air_final: float32 [128, 2880, 128], P('lat', 'lon')
- sea_final: float32 [128, 2880], P(('lat', 'lon'))
Inputs may be any that keep to these rules, and one draw needn't show every extreme that they name: cutoffs holds the rows in the order of the filtered rows; some row keeps exactly 127.
All inputs are finite; a program needn't handle non-finite values. No bound on the sum of `land_sea` on one device may be relied on, other than what follows from the above.
Results may differ from a plain program's by a relative error of at most 0.0001.
Values sent between devices are 32-bit elements; how exact they have to be, the bound alone decides.
A program may use at most 128 MiB of HBM per device.

v0:
```python
import math

import jax
import jax.numpy as jnp
from jax import lax
from jax.sharding import PartitionSpec as P

NLON = 2880
NPOLE = 16
KMAX = 127
STEPS = 6


diffusion_rate = 0.1
air_gain = 0.5
ocean_gain = 0.3
ocean_diffusion = 0.2
sea_coef = 0.5
land_coef = 0.15


def with_halo(array, sides, width, wrap):
    for axis, dim in sides:
        size, length = (lax.axis_size(axis), array.shape[dim])
        up = [(i, (i + 1) % size) for i in range(size if wrap else size - 1)]
        down = [(j, i) for i, j in up]
        last = lax.slice_in_dim(array, length - width, length, axis=dim)
        leading = lax.slice_in_dim(array, 0, width, axis=dim)
        before = lax.ppermute(last, axis, up)
        after = lax.ppermute(leading, axis, down)
        array = jnp.concatenate([before, array, after], axis=dim)
    return array


def horizontal(air_temp, courant):
    lat_padded = with_halo(air_temp, (("lat", 0),), 1, False)
    lon_padded = with_halo(air_temp, (("lon", 1),), 1, True)
    north_cell = lat_padded[:-2]
    south_cell = lat_padded[2:]
    west_cell = lon_padded[:, :-2]
    east_cell = lon_padded[:, 2:]
    laplace = north_cell + south_cell + east_cell + west_cell - 4.0 * air_temp
    return air_temp + diffusion_rate * laplace - 0.5 * courant * (east_cell - west_cell)


def tables(first_column, count):
    wavenum = jnp.arange(KMAX + 1, dtype=jnp.int32)
    columns = first_column + jnp.arange(count, dtype=jnp.int32)
    phase = (columns[:, None] * wavenum[None, :] % NLON).astype(jnp.float32) * (
        2.0 * math.pi / NLON
    )
    return (jnp.cos(phase), jnp.sin(phase))


def spectra(polar_rows, cosine, sine_table):
    real_part = jnp.einsum("pcl,ck->pkl", polar_rows, cosine, precision=lax.Precision.HIGHEST)
    imag_part = jnp.einsum("pcl,ck->pkl", polar_rows, sine_table, precision=lax.Precision.HIGHEST)
    return (real_part, imag_part)


def inverse(real_part, imag_part, cutoff, cosine, sine_table):
    wavenum = jnp.arange(KMAX + 1, dtype=jnp.int32)
    weights = (
        jnp.where(
            wavenum[None, :] <= cutoff[:, None], jnp.where(wavenum[None, :] == 0, 1.0, 2.0), 0.0
        )
        / NLON
    )
    weights = weights[:, :, None]
    return jnp.einsum(
        "pkl,ck->pcl", real_part * weights, cosine, precision=lax.Precision.HIGHEST
    ) + jnp.einsum("pkl,ck->pcl", imag_part * weights, sine_table, precision=lax.Precision.HIGHEST)


def ocean_step(sea_temp, flux_ocean):
    padded = with_halo(sea_temp, ((("lat", "lon"), 0),), 1, False)
    laplace = (
        padded[:-2]
        + padded[2:]
        + jnp.roll(sea_temp, 1, axis=1)
        + jnp.roll(sea_temp, -1, axis=1)
        - 4.0 * sea_temp
    )
    return sea_temp - ocean_gain * flux_ocean + ocean_diffusion * laplace


def local(air_temp, sea_temp, land_sea, courant, vertical_mix, cutoffs):
    row_count, col_count, levels = air_temp.shape
    band_index = lax.axis_index("lat")
    is_north = band_index == 0
    is_south = band_index == lax.axis_size("lat") - 1
    col_start = lax.axis_index("lon") * col_count
    cosine, sine_table = tables(col_start, col_count)
    exchange_coef = jnp.where(land_sea == 1, sea_coef, land_coef)
    for step_index in range(STEPS):
        sea_near = lax.all_to_all(sea_temp, "lon", split_axis=1, concat_axis=0, tiled=True)
        advanced = horizontal(air_temp, courant)
        polar_rows = jnp.where(is_north, advanced[:NPOLE], advanced[row_count - NPOLE :])
        cutoff = jnp.where(is_north, cutoffs[:NPOLE], cutoffs[NPOLE:])
        real_part, imag_part = spectra(polar_rows, cosine, sine_table)
        real_part, imag_part = lax.psum((real_part, imag_part), "lon")
        filtered = inverse(real_part, imag_part, cutoff, cosine, sine_table)
        north_block = jnp.concatenate([filtered, advanced[NPOLE:]], 0)
        south_block = jnp.concatenate([advanced[: row_count - NPOLE], filtered], 0)
        advanced = jnp.where(is_north, north_block, jnp.where(is_south, south_block, advanced))
        mixed = jnp.dot(advanced.reshape(-1, levels), vertical_mix, precision=lax.Precision.HIGHEST)
        air_next = advanced + mixed.reshape(advanced.shape)
        heat_flux = exchange_coef * (sea_near - air_next[:, :, 0])
        air_temp = air_next.at[:, :, 0].add(air_gain * heat_flux)
        flux_ocean = lax.all_to_all(heat_flux, "lon", split_axis=0, concat_axis=1, tiled=True)
        sea_temp = ocean_step(sea_temp, flux_ocean)
    return (air_temp, sea_temp)


def solution(mesh):
    placed = (P("lat", "lon", None), P(("lat", "lon"), None), P("lat", "lon"), P(), P(), P())
    return jax.shard_map(
        local,
        mesh=mesh,
        in_specs=placed,
        out_specs=(P("lat", "lon", None), P(("lat", "lon"), None)),
        check_vma=False,
    )
```

profile of v0, /device:TPU:0, one launch (start us, length us, event | category | flops | bytes accessed | tf_op | source)
XLA Modules:
  0.0 2430.2 jit_solution(3091324834380990453)
XLA Ops:
  12.8 9.5 collective-permute-start.2
  43.3 347.9 %all-reduce.23.cloned.1.call-done = (f32[16,128,128]{2,1,0:T(8,128)}, f32[16,128,128]{2,1,0:T(8,128)}) async-done(((f32[16,128,128]{2,1,0:T(8,128)}, f32[16,128,128]{2,1,0:T(8,128)}), (f32[16,128,128]{2,1,0:T(8,128)}, f32[16,128,128]{2,1,0:T(8,128)})) %all-reduce.23.cloned.1.call-update) | async-done | bytes 2097168 | tf_op jit(solution)/shard_map/psum | solution.py:101
  401.1 9.9 scatter-add.20
  438.5 11.4 all-to-all-start.1
  450.5 9.2 all-to-all-done.1
  467.3 323.1 %all-reduce.21.cloned.1.call-done = (f32[16,128,128]{2,1,0:T(8,128)}, f32[16,128,128]{2,1,0:T(8,128)}) async-done(((f32[16,128,128]{2,1,0:T(8,128)}, f32[16,128,128]{2,1,0:T(8,128)}), (f32[16,128,128]{2,1,0:T(8,128)}, f32[16,128,128]{2,1,0:T(8,128)})) %all-reduce.21.cloned.1.call-update) | async-done | bytes 2097168 | tf_op jit(solution)/shard_map/psum | solution.py:101
  800.3 9.9 scatter-add.21
  837.8 11.4 all-to-all-start.3
  849.8 9.2 all-to-all-done.3
  866.6 323.1 %all-reduce.19.cloned.1.call-done = (f32[16,128,128]{2,1,0:T(8,128)}, f32[16,128,128]{2,1,0:T(8,128)}) async-done(((f32[16,128,128]{2,1,0:T(8,128)}, f32[16,128,128]{2,1,0:T(8,128)}), (f32[16,128,128]{2,1,0:T(8,128)}, f32[16,128,128]{2,1,0:T(8,128)})) %all-reduce.19.cloned.1.call-update) | async-done | bytes 2097168 | tf_op jit(solution)/shard_map/psum | solution.py:101
  1199.5 9.9 scatter-add.24
  1236.8 11.4 all-to-all-start.5
  1248.8 9.2 all-to-all-done.5
  1265.6 323.5 %all-reduce.17.cloned.1.call-done = (f32[16,128,128]{2,1,0:T(8,128)}, f32[16,128,128]{2,1,0:T(8,128)}) async-done(((f32[16,128,128]{2,1,0:T(8,128)}, f32[16,128,128]{2,1,0:T(8,128)}), (f32[16,128,128]{2,1,0:T(8,128)}, f32[16,128,128]{2,1,0:T(8,128)})) %all-reduce.17.cloned.1.call-update) | async-done | bytes 2097168 | tf_op jit(solution)/shard_map/psum | solution.py:101
  1598.9 9.9 scatter-add.25
  1636.3 11.4 all-to-all-start.7
  1648.3 9.2 all-to-all-done.7
  1665.0 323.1 %all-reduce.15.cloned.1.call-done = (f32[16,128,128]{2,1,0:T(8,128)}, f32[16,128,128]{2,1,0:T(8,128)}) async-done(((f32[16,128,128]{2,1,0:T(8,128)}, f32[16,128,128]{2,1,0:T(8,128)}), (f32[16,128,128]{2,1,0:T(8,128)}, f32[16,128,128]{2,1,0:T(8,128)})) %all-reduce.15.cloned.1.call-update) | async-done | bytes 2097168 | tf_op jit(solution)/shard_map/psum | solution.py:101
  1998.0 9.9 scatter-add.26
  2039.3 9.2 all-to-all-done.9
  2054.6 10.0 all-to-all-start.10
  2066.6 323.7 %all-reduce.13.cloned.1.call-done = (f32[16,128,128]{2,1,0:T(8,128)}, f32[16,128,128]{2,1,0:T(8,128)}) async-done(((f32[16,128,128]{2,1,0:T(8,128)}, f32[16,128,128]{2,1,0:T(8,128)}), (f32[16,128,128]{2,1,0:T(8,128)}, f32[16,128,128]{2,1,0:T(8,128)})) %all-reduce.13.cloned.1.call-update) | async-done | bytes 2097168 | tf_op jit(solution)/shard_map/psum | solution.py:101
  2396.9 8.7 all-to-all-start.11
  2408.9 9.9 scatter-add.29
  (264 shorter events, 270.6 us)
Async XLA Ops:
  7.2 384.0 %all-reduce.23.cloned.1.call-start = ((), (), s32[]{:S(2)}) async-start(), calls=%async_computation.17 | async-start | bytes 4194304 | tf_op jit(solution)/shard_map/psum | solution.py:101
  37.9 359.2 %all-to-all-start = ((f32[1,32,90]{2,0,1:T(1,128)}), f32[1,32,90]{2,0,1:T(1,128)S(1)}, u32[]{:S(2)}, u32[]{:S(2)}) async-start(f32[1,32,90]{2,0,1:T(1,128)} %all_to_all.132), calls=%async_computation | async-start | bytes 32768 | tf_op jit(solution)/shard_map/all_to_all | solution.py:96
  41.8 748.6 %all-reduce.21.cloned.1.call-start = ((), (), s32[]{:S(2)}) async-start(), calls=%async_computation.16 | async-start | bytes 4194304 | tf_op jit(solution)/shard_map/psum | solution.py:101
  435.8 24.1 collective-permute-start.8
  437.1 22.8 collective-permute-start.9
  462.1 334.2 %all-to-all-start.2 = ((f32[1,32,90]{2,0,1:T(1,128)}), f32[1,32,90]{2,0,1:T(1,128)S(1)}, u32[]{:S(2)}, u32[]{:S(2)}) async-start(f32[1,32,90]{2,0,1:T(1,128)} %all_to_all.137), calls=%async_computation.2 | async-start | bytes 32768 | tf_op jit(solution)/shard_map/all_to_all | solution.py:96
  465.9 723.7 %all-reduce.19.cloned.1.call-start = ((), (), s32[]{:S(2)}) async-start(), calls=%async_computation.15 | async-start | bytes 4194304 | tf_op jit(solution)/shard_map/psum | solution.py:101
  835.1 24.1 collective-permute-start.14
  836.4 22.8 collective-permute-start.15
  861.4 334.2 %all-to-all-start.4 = ((f32[1,32,90]{2,0,1:T(1,128)}), f32[1,32,90]{2,0,1:T(1,128)S(1)}, u32[]{:S(2)}, u32[]{:S(2)}) async-start(f32[1,32,90]{2,0,1:T(1,128)} %all_to_all.142), calls=%async_computation.4 | async-start | bytes 32768 | tf_op jit(solution)/shard_map/all_to_all | solution.py:96
  865.2 723.9 %all-reduce.17.cloned.1.call-start = ((), (), s32[]{:S(2)}) async-start(), calls=%async_computation.14 | async-start | bytes 4194304 | tf_op jit(solution)/shard_map/psum | solution.py:101
  1234.1 24.1 collective-permute-start.20
  1260.4 334.6 %all-to-all-start.6 = ((f32[1,32,90]{2,0,1:T(1,128)}), f32[1,32,90]{2,0,1:T(1,128)S(1)}, u32[]{:S(2)}, u32[]{:S(2)}) async-start(f32[1,32,90]{2,0,1:T(1,128)} %all_to_all.147), calls=%async_computation.6 | async-start | bytes 32768 | tf_op jit(solution)/shard_map/all_to_all | solution.py:96
  1264.2 723.9 %all-reduce.15.cloned.1.call-start = ((), (), s32[]{:S(2)}) async-start(), calls=%async_computation.13 | async-start | bytes 4194304 | tf_op jit(solution)/shard_map/psum | solution.py:101
  1633.6 24.1 collective-permute-start.26
  1634.9 22.8 collective-permute-start.27
  1659.8 334.2 %all-to-all-start.8 = ((f32[1,32,90]{2,0,1:T(1,128)}), f32[1,32,90]{2,0,1:T(1,128)S(1)}, u32[]{:S(2)}, u32[]{:S(2)}) async-start(f32[1,32,90]{2,0,1:T(1,128)} %all_to_all.152), calls=%async_computation.8 | async-start | bytes 32768 | tf_op jit(solution)/shard_map/all_to_all | solution.py:96
  1663.7 726.7 %all-reduce.13.cloned.1.call-start = ((), (), s32[]{:S(2)}) async-start(), calls=%async_computation.12 | async-start | bytes 4194304 | tf_op jit(solution)/shard_map/psum | solution.py:101
  2017.7 31.0 %collective-permute-start.32 = (f32[1,2880]{1,0:T(1,128)S(1)}, f32[1,2880]{1,0:T(1,128)S(1)}, u32[]{:S(2)}, u32[]{:S(2)}) collective-permute-start(f32[1,2880]{1,0:T(1,128)S(1)} %get-tuple-element.121), channel_id=1, source_target_pairs={{0,1},{1,2},{2,3},{3,4},{4,5},{5,6},{6,7},{7,8},{8,9},{9,10},{10,1... | collective-permute-start | bytes 34568 | tf_op jit(solution)/shard_map/ppermute | solution.py:29
  2019.1 29.5 %collective-permute-start.33 = (f32[1,2880]{1,0:T(1,128)S(1)}, f32[1,2880]{1,0:T(1,128)S(1)}, u32[]{:S(2)}, u32[]{:S(2)}) collective-permute-start(f32[1,2880]{1,0:T(1,128)S(1)} %get-tuple-element.121), channel_id=1, source_target_pairs={{1,0},{2,1},{3,2},{4,3},{5,4},{6,5},{7,6},{8,7},{9,8},{10,9},{11,1... | collective-permute-start | bytes 34568 | tf_op jit(solution)/shard_map/ppermute | solution.py:30
  2050.1 370.9 %collective-permute-start.34 = (f32[1,2880]{1,0:T(1,128)S(1)}, f32[1,2880]{1,0:T(1,128)S(1)}, u32[]{:S(2)}, u32[]{:S(2)}) collective-permute-start(f32[1,2880]{1,0:T(1,128)S(1)} %get-tuple-element.117), channel_id=1, source_target_pairs={{0,1},{1,2},{2,3},{3,4},{4,5},{5,6},{6,7},{7,8},{8,9},{9,10},{10,1... | collective-permute-start | bytes 34568 | tf_op jit(solution)/shard_map/ppermute | solution.py:29
  2052.6 368.4 %collective-permute-start.35 = (f32[1,2880]{1,0:T(1,128)S(1)}, f32[1,2880]{1,0:T(1,128)S(1)}, u32[]{:S(2)}, u32[]{:S(2)}) collective-permute-start(f32[1,2880]{1,0:T(1,128)S(1)} %get-tuple-element.117), channel_id=1, source_target_pairs={{1,0},{2,1},{3,2},{4,3},{5,4},{6,5},{7,6},{8,7},{9,8},{10,9},{11,1... | collective-permute-start | bytes 34568 | tf_op jit(solution)/shard_map/ppermute | solution.py:30
  2054.6 341.7 %all-to-all-start.10 = ((f32[1,32,90]{2,0,1:T(1,128)}), f32[1,32,90]{2,0,1:T(1,128)S(1)}, u32[]{:S(2)}, u32[]{:S(2)}) async-start(f32[1,32,90]{2,0,1:T(1,128)} %all_to_all.157), calls=%async_computation.10 | async-start | bytes 32768 | tf_op jit(solution)/shard_map/all_to_all | solution.py:96
  2396.9 23.9 all-to-all-start.11
  (53 other events, 908.3 us)
Sparse Core Ops, SparseCore 0:
  37.3 353.8 all-reduce.22
  436.0 354.3 all-reduce.20
  835.3 354.3 all-reduce.18
  1234.3 354.7 all-reduce.16
  1633.7 354.3 all-reduce.14
  2032.6 357.6 all-reduce.12
where the time goes:
time: 2440 us; the launch traced here: 2430 us
  waiting for transfers between devices  2060 us (84%)
  starting transfers between devices  168 us (7%)
  local copies, waits for them, and re-layouts  96.9 us (4%)
  matrix products  57.8 us (2%)
  other arithmetic  27.3 us (1%)
    psum x6, waiting for transfers between devices, local(): real_part, imag_part = lax.psum((real_part, imag_part), 'lon')  1960 us
    ppermute x18, starting transfers between devices, with_halo(): after = lax.ppermute(leading, axis, down)  60.6 us
    all_to_all x6, starting transfers between devices, local(): lax.all_to_all(heat_flux, 'lon', split_axis=0, concat_axis=1, tiled=True)  60.4 us
    scatter-add x6, local copies, waits for them, and re-layouts, local(): air_temp = air_next.at[:, :, 0].add(air_gain * heat_flux)  59.7 us
  transfers between devices with their start and end apart: 54, of which 23 were waited for; matrix products, arithmetic and copies ran while one was open for 3% of the time, Pallas kernels for 0%

commit v1 on v0

v1 whole, which is shorter than its diff:
```python
import functools

import jax
import jax.numpy as jnp
import ml_dtypes
import numpy as np
from jax import lax
from jax.experimental import pallas as pl
from jax.experimental.pallas import tpu as pltpu
from jax.sharding import PartitionSpec as P

STEPS = 6
NPOLE = 16
ROWS = 32
COLS = 90
KW = 128
LEV = 128
HALO = 6
FRAMES = 49
WIDE = 120
Q0, QN = 8, 104
SPEC = NPOLE + HALO
PACK = 24

f32, bf16 = jnp.float32, jnp.bfloat16
MESH = pl.DeviceIdType.MESH


def split(x):
    hi = x.astype(bf16)
    return hi, (x - hi.astype(f32)).astype(bf16)


def dot(a, b):
    return jnp.dot(a, b, preferred_element_type=f32)


def dot3(a, b):
    return dot(a[0], b[0]) + dot(a[1], b[0]) + dot(a[0], b[1])


def np_split(x):
    x = x.astype(np.float32)
    hi = x.astype(ml_dtypes.bfloat16)
    lo = (x - hi.astype(np.float32)).astype(ml_dtypes.bfloat16)
    return np.stack([hi, lo])


def tables(nl):
    nlon = nl * COLS
    k = np.arange(KW)

    def fwd(c):
        ang = (c[..., None] * k % nlon) * (2.0 * np.pi / nlon)
        return np.concatenate([np.cos(ang), np.sin(ang)], -1)

    weight = np.where(k == 0, 1.0, 2.0) / nlon
    weight = np.concatenate([weight, weight])
    d = np.arange(nl)[:, None]
    c = np.arange(96)[None]
    full = np.where((c < COLS)[..., None], fwd(d * COLS + c), 0.0)
    own = np.moveaxis(np_split(full.transpose(0, 2, 1)), 0, 1)
    q = np.arange(QN)[None]
    inv = np.moveaxis(np_split(fwd((d * COLS + q - 8) % nlon) * weight), 0, 1)
    packed = full.reshape(nl, 4, PACK, 256).transpose(1, 3, 0, 2).reshape(4, 256, nl * PACK)
    step = 2.0 * np.pi / nlon
    wave = np.stack([0.6 + 0.2 * np.cos(k * step), np.sin(k * step)])
    wave = np.broadcast_to(wave[:, :, None], (2, KW, LEV)).astype(np.float32)
    return own, inv, np_split(packed), wave


def kernel(nl, a_ref, seaw_ref, coef_ref, cour_ref, vmix_ref, cut_ref, own_hbm, inv_hbm, ct_hbm,
           wave_ref, out_ref, seaout_ref, fa, fb, sa, sb, part, rsb, fx, fp, halo, coefr, sear,
           seab, seaf, seafin, sendx, recvx, own, inv, ct, vb, mt, a0t, coeft, st0, st1, fluxt,
           s0t, wv, tsem, asem, csem, seas, searow, xsem, rssem, agsem, fxs, fins):
    lat, lon = lax.axis_index("lat"), lax.axis_index("lon")
    polar = jnp.logical_or(lat == 0, lat == 3)
    flip = lat == 3
    ko = 2 * KW // nl
    rp = ROWS // nl
    lane = lax.broadcasted_iota(jnp.int32, (QN, LEV), 1)

    def natural(m):
        return jnp.where(flip, ROWS - 1 - m, m)

    def peers(body):
        def one(i, carry):
            body(lax.rem(lon + i, nl))
            return carry
        lax.fori_loop(1, nl, one, 0)

    def wait_bytes(ref, sem):
        pltpu.make_async_copy(ref, ref, sem).wait()

    def to_lon(src, dst, ssem, rsem, peer):
        return pltpu.make_async_remote_copy(src, dst, ssem, rsem, device_id={"lon": peer},
                                            device_id_type=MESH)

    loads = [
        pltpu.make_async_copy(own_hbm.at[lon], own, tsem.at[0]),
        pltpu.make_async_copy(inv_hbm.at[lon], inv, tsem.at[1]),
        pltpu.make_async_copy(ct_hbm, ct, tsem.at[2]),
    ]

    @pl.when(polar)
    def _():
        for load in loads:
            load.start()

    barrier = pltpu.get_barrier_semaphore()
    peers(lambda p: pl.semaphore_signal(barrier, inc=1, device_id={"lon": p}, device_id_type=MESH))

    @pl.when(lat < 3)
    def _():
        pl.semaphore_signal(barrier, inc=1, device_id={"lat": lat + 1}, device_id_type=MESH)

    @pl.when(lat > 0)
    def _():
        pl.semaphore_signal(barrier, inc=1, device_id={"lat": lat - 1}, device_id_type=MESH)

    pl.semaphore_wait(barrier, nl - 1 + jnp.where(polar, 1, 2))

    side = jnp.where(lat == 2, 1, 0)

    def lat_sends(src_ref, dst_ref, sems):
        def make(src, s, i, which, to):
            return pltpu.make_async_remote_copy(
                src_ref.at[src], dst_ref.at[s, i], sems.at[which], sems.at[2 + s],
                device_id={"lat": to}, device_id_type=MESH)

        @pl.when(lat < 3)
        def _():
            for i in range(HALO):
                make(jnp.where(lat == 2, ROWS - 1 - i, ROWS - HALO + i), side, i, 0, lat + 1).start()

        @pl.when(lat > 0)
        def _():
            for i in range(HALO):
                make(i, 1, i, 1, lat - 1).start()

    def lat_recvs(dst_ref, sems):
        wait_bytes(dst_ref.at[1], sems.at[3])

        @pl.when(jnp.logical_not(polar))
        def _():
            wait_bytes(dst_ref.at[0], sems.at[2])

    def lat_sent(dst_ref, sems):
        @pl.when(lat < 3)
        def _():
            wait_bytes(dst_ref.at[0], sems.at[0])

        @pl.when(lat > 0)
        def _():
            wait_bytes(dst_ref.at[0], sems.at[1])

    peers(lambda p: to_lon(seaw_ref.at[p], seab.at[pl.ds(rp * lon, rp)], seas.at[0], seas.at[1], p).start())
    lat_sends(coef_ref, coefr, csem)
    lat_sends(a_ref, halo, asem)

    def own_sea(i, carry):
        seab[rp * lon + i] = seaw_ref[lon, i]
        return carry
    lax.fori_loop(0, rp, own_sea, 0)

    def clear(f, carry):
        z = jnp.zeros((8, LEV), f32)
        fa[f, pl.ds(0, 8), :] = z
        fa[f, pl.ds(WIDE - 16, 8), :] = z
        fa[f, pl.ds(WIDE - 8, 8), :] = z
        fb[f, pl.ds(0, 8), :] = z
        fb[f, pl.ds(WIDE - 8, 8), :] = z
        return carry
    lax.fori_loop(0, FRAMES, clear, 0)
    for f in (0, 1, 46, 47):
        fa[f] = jnp.zeros((WIDE, LEV), f32)
        fb[f] = jnp.zeros((WIDE, LEV), f32)
    fa[48] = jnp.zeros((WIDE, LEV), f32)
    fb[48] = jnp.zeros((WIDE, LEV), f32)

    def fill(m, carry):
        fa[m + 8, pl.ds(16, COLS), :] = a_ref[natural(m)]
        return carry
    lax.fori_loop(0, ROWS, fill, 0)

    @pl.when(polar)
    def _():
        loads[0].wait()
        tab = (own[0], own[1])

        def transform(i, carry):
            f = 8 + 2 * i
            rows = jnp.concatenate([fa[f, pl.ds(16, 96), :], fa[f + 1, pl.ds(16, 96), :]], 1)
            res = dot3(tab, split(rows))
            part[2 * i] = res[:, :LEV]
            part[2 * i + 1] = res[:, LEV:]
            return carry
        lax.fori_loop(0, SPEC // 2, transform, 0)

        def chunk(p):
            return part.at[:, pl.ds(pl.multiple_of(p * ko, 8), ko), :]
        peers(lambda p: to_lon(chunk(p), rsb.at[lon], rssem.at[0], rssem.at[1], p).start())
        rsb[lon] = part[:, pl.ds(pl.multiple_of(lon * ko, 8), ko), :]

    col0 = jnp.broadcast_to(vmix_ref[:, 0:1], (LEV, LEV))
    rowid = lax.broadcasted_iota(jnp.int32, (LEV, LEV), 0)
    both = jnp.concatenate([vmix_ref[...], col0 + jnp.where(rowid == 0, 1.0, 0.0)], 1)
    bhi, blo = split(both)
    vb[0, pl.ds(0, LEV), :] = bhi
    vb[0, pl.ds(LEV, LEV), :] = bhi
    vb[1, pl.ds(0, LEV), :] = blo
    vb[1, pl.ds(LEV, LEV), :] = jnp.zeros_like(blo)

    def levels(x):
        both = jnp.concatenate(split(x), 1)
        res = dot(both, vb[0]) + dot(both, vb[1])
        return x + res[:, :LEV], res[:, LEV:]

    cour = cour_ref[...]
    east = 0.1 - 0.5 * cour
    west = 0.1 + 0.5 * cour
    wv[0] = wave_ref[0]
    wv[1] = wave_ref[1] * cour

    lat_recvs(halo, asem)
    for i in range(HALO):
        fa[40 + i, pl.ds(16, COLS), :] = halo[1, i]

    @pl.when(jnp.logical_not(polar))
    def _():
        for i in range(HALO):
            fa[2 + i, pl.ds(16, COLS), :] = halo[0, i]

    @pl.when(polar)
    def _():
        for i in range(HALO):
            fa[2 + i] = jnp.zeros((WIDE, LEV), f32)
            fb[2 + i] = jnp.zeros((WIDE, LEV), f32)

    def gather_rows(own_of, got):
        mt[...] = jnp.zeros_like(mt)

        def put(m, carry):
            mt[pl.ds(m + 8, 1), :] = own_of(m)
            return carry
        lax.fori_loop(0, ROWS, put, 0)
        for i in range(HALO):
            mt[40 + i:41 + i, :] = got[1, i]

        @pl.when(jnp.logical_not(polar))
        def _():
            for i in range(HALO):
                mt[2 + i:3 + i, :] = got[0, i]
        return mt[...].T

    lat_recvs(coefr, csem)
    fa[48, pl.ds(16, COLS), :] = gather_rows(lambda m: coef_ref[natural(m)], coefr)[:COLS]

    def pack(f, carry):
        sendx[0, f] = fa[f, pl.ds(16 + COLS - 8, 8), :]
        sendx[1, f] = fa[f, pl.ds(16, 8), :]
        return carry
    lax.fori_loop(2, FRAMES, pack, 0)
    zero = jnp.zeros((8, LEV), f32)
    for s in range(2):
        for f in range(2):
            sendx[s, f] = zero
    ahead = lax.rem(lon + 1, nl)
    behind = lax.rem(lon + nl - 1, nl)
    to_east = to_lon(sendx.at[0], recvx.at[0], xsem.at[0], xsem.at[2], ahead)
    to_west = to_lon(sendx.at[1], recvx.at[1], xsem.at[1], xsem.at[3], behind)
    to_east.start()
    to_west.start()

    wait_bytes(seab.at[pl.ds(0, ROWS - rp)], seas.at[1])
    lat_sends(seab, sear, searow)
    lat_recvs(sear, searow)
    st0[...] = jnp.zeros_like(st0)
    st1[...] = jnp.zeros_like(st1)
    st0[pl.ds(Q0, QN), :] = gather_rows(lambda m: seab[natural(m)], sear)[:QN]

    to_east.wait_recv()
    to_west.wait_recv()

    def unpack(f, carry):
        fa[f, pl.ds(8, 8), :] = recvx[0, f]
        fa[f, pl.ds(16 + COLS, 8), :] = recvx[1, f]
        return carry
    lax.fori_loop(2, FRAMES, unpack, 0)
    coeft[...] = fa[48, pl.ds(Q0, QN), :]

    @pl.when(polar)
    def _():
        sa[0] = jnp.zeros((2 * KW, LEV), f32)
        sb[0] = jnp.zeros((2 * KW, LEV), f32)
        wait_bytes(rsb.at[pl.ds(0, nl - 1)], rssem.at[1])

        def add_up(r, carry):
            total = rsb[0, r]
            for d in range(1, nl):
                total = total + rsb[d, r]
            sa[r + 1, pl.ds(pl.multiple_of(lon * ko, 8), ko), :] = total
            return carry
        lax.fori_loop(0, SPEC, add_up, 0)
        mine = sa.at[pl.ds(1, SPEC), pl.ds(pl.multiple_of(lon * ko, 8), ko), :]
        peers(lambda p: to_lon(mine, mine, agsem.at[0], agsem.at[1], p).start())

    first = jnp.where(polar, 5, 0)
    lane_ok = jnp.logical_or(lane >= 8, jnp.logical_not(polar))
    kid = lax.broadcasted_iota(jnp.int32, (KW, LEV), 0)
    klane = lax.broadcasted_iota(jnp.int32, (2 * KW, LEV), 1)
    glane = lax.broadcasted_iota(jnp.int32, (PACK, LEV), 1) // 32

    for t in range(1, STEPS + 1):
        src, dst = (fa, fb) if t % 2 else (fb, fa)
        ssrc, sdst = (sa, sb) if t % 2 else (sb, sa)
        sea, sea_next = (st0, st1) if t % 2 else (st1, st0)

        def grid_rows(i, acc):
            adv = []
            for j in range(4):
                f = 4 * i + 2 + j
                mid = pl.ds(Q0, QN)
                adv.append(0.6 * src[f, mid, :] + 0.1 * (src[f - 1, mid, :] + src[f + 1, mid, :])
                           + east * src[f, pl.ds(Q0 + 1, QN), :] + west * src[f, pl.ds(Q0 - 1, QN), :])
            new, low = levels(jnp.concatenate(adv, 0))
            for j in range(4):
                f = 4 * i + 2 + j
                dst[f, pl.ds(Q0, QN), :] = new[j * QN:(j + 1) * QN]
                acc = jnp.where(lane == f, low[j * QN:(j + 1) * QN], acc)
            return acc
        a0t[...] = lax.fori_loop(first, 11, grid_rows, jnp.zeros((QN, LEV), f32))

        @pl.when(polar)
        def _():
            if t == 1:
                loads[1].wait()
                loads[2].wait()
                wait_bytes(sa.at[pl.ds(1, SPEC), pl.ds(0, ko * (nl - 1)), :], agsem.at[1])
            else:
                wait_bytes(fx.at[t - 2, pl.ds(0, nl - 1)], fxs.at[t - 2, 1])
                got = split(fx[t - 2].reshape(nl * PACK, LEV))
                hat = jnp.zeros((2 * KW, LEV), f32)
                for g in range(4):
                    res = dot3((ct[0, g], ct[1, g]), got)
                    hat = hat + jnp.where(klane // 32 == g, res, 0.0)
                hat = hat + pltpu.roll(hat, 64, 1)
                hat = hat + pltpu.roll(hat, 32, 1)

                def add_flux(r, carry):
                    turned = pltpu.roll(hat, lax.rem(LEV - r, LEV), 1)
                    ssrc[r + 1] = ssrc[r + 1] + jnp.where(klane == 0, 0.5 * turned, 0.0)
                    return carry
                lax.fori_loop(0, SPEC + 1 - t, add_flux, 0)

            def waves(r, acc):
                here, up, down = ssrc[r + 1], ssrc[r], ssrc[r + 2]
                re, im = here[:KW], here[KW:]
                near = 0.1 * (up + down)
                c, s = wv[0], wv[1]
                are = c * re - s * im + near[:KW]
                aim = c * im + s * re + near[KW:]
                cut = jnp.where(r < NPOLE, cut_ref[jnp.where(flip, 2 * NPOLE - 1 - jnp.minimum(r, NPOLE - 1), jnp.minimum(r, NPOLE - 1))], KW)
                keep = kid <= cut
                adv = jnp.concatenate([jnp.where(keep, are, 0.0), jnp.where(keep, aim, 0.0)], 0)
                new, low = levels(adv)
                sdst[r + 1] = new
                return jnp.where(klane == r + 8, low, acc)
            s0t[...] = lax.fori_loop(0, SPEC - t, waves, jnp.zeros((2 * KW, LEV), f32))
            res = dot3((inv[0], inv[1]), split(jnp.concatenate([s0t[...], sdst[NPOLE]], 1)))
            filtered = jnp.logical_and(lane >= 8, lane < 8 + NPOLE)
            a0t[...] = jnp.where(filtered, res[:, :LEV], a0t[...])
            dst[7 + NPOLE, pl.ds(Q0, QN), :] = res[:, LEV:]
            if t == 1:
                wait_bytes(sa.at[pl.ds(1, SPEC), pl.ds(0, ko * (nl - 1)), :], agsem.at[0])

        now = sea[pl.ds(Q0, QN), :]
        flux = coeft[...] * (now - a0t[...])
        fluxt[...] = flux
        around = (pltpu.roll(now, 1, 1) + pltpu.roll(now, LEV - 1, 1)
                  + sea[pl.ds(Q0 - 1, QN), :] + sea[pl.ds(Q0 + 1, QN), :])
        later = now - 0.3 * flux + 0.2 * (around - 4.0 * now)
        sea_next[pl.ds(Q0, QN), :] = jnp.where(lane_ok, later, 0.0)

        if t < STEPS:
            @pl.when(polar)
            def _():
                msg = jnp.zeros((PACK, LEV), f32)
                for g in range(4):
                    turned = pltpu.roll(fluxt[pl.ds(8 + PACK * g, PACK), :], (32 * g - 8) % LEV, 1)
                    msg = jnp.where(glane == g, turned, msg)
                fp[t - 1] = msg
                fx[t - 1, lon] = msg
                peers(lambda p: to_lon(fp.at[t - 1], fx.at[t - 1, lon], fxs.at[t - 1, 0], fxs.at[t - 1, 1], p).start())

        def warm(f, carry):
            turned = pltpu.roll(fluxt[...], LEV - f, 1)
            dst[f, pl.ds(Q0, QN), :] = dst[f, pl.ds(Q0, QN), :] + jnp.where(lane == 0, 0.5 * turned, 0.0)
            return carry
        lax.fori_loop(jnp.where(polar, 23, 2), 46, warm, 0)

    last, slast, sea = fa, sa, st0

    mt[...] = sea[pl.ds(16, LEV), :].T

    def put_row(n, carry):
        seaf[n] = mt[pl.ds(natural(n) + 8, 1), :]
        return carry
    lax.fori_loop(0, ROWS, put_row, 0)
    peers(lambda p: to_lon(seaf.at[pl.ds(rp * p, rp)], seafin.at[lon], fins.at[0], fins.at[1], p).start())

    def own_fin(i, carry):
        seafin[lon, i] = seaf[rp * lon + i]
        return carry
    lax.fori_loop(0, rp, own_fin, 0)

    @pl.when(polar)
    def _():
        tab = (inv[0], inv[1])

        def give(i, carry):
            res = dot3(tab, split(jnp.concatenate([slast[2 * i + 1], slast[2 * i + 2]], 1)))
            for j in range(2):
                turned = pltpu.roll(fluxt[...], LEV - 8 - (2 * i + j), 1)
                value = res[:, j * LEV:(j + 1) * LEV] + jnp.where(lane == 0, 0.5 * turned, 0.0)
                out_ref[natural(2 * i + j)] = value[8:8 + COLS]
            return carry
        lax.fori_loop(0, NPOLE // 2, give, 0)

    def give_grid(m, carry):
        out_ref[natural(m)] = last[m + 8, pl.ds(16, COLS), :]
        return carry
    lax.fori_loop(jnp.where(polar, NPOLE, 0), ROWS, give_grid, 0)

    wait_bytes(seafin.at[pl.ds(0, nl - 1)], fins.at[1])
    seaout_ref[...] = seafin[...]

    wait_bytes(seafin.at[pl.ds(0, nl - 1)], fins.at[0])
    wait_bytes(seab.at[pl.ds(0, ROWS - rp)], seas.at[0])
    lat_sent(halo, asem)
    lat_sent(coefr, csem)
    lat_sent(sear, searow)
    to_east.wait_send()
    to_west.wait_send()

    @pl.when(polar)
    def _():
        wait_bytes(rsb.at[pl.ds(0, nl - 1)], rssem.at[0])
        for t in range(STEPS - 1):
            wait_bytes(fx.at[t, pl.ds(0, nl - 1)], fxs.at[t, 0])


def local(nl, consts, air, sea, land, courant, vmix, cutoffs):
    rp = ROWS // nl
    ko = 2 * KW // nl
    blocks = sea.reshape(rp, nl, COLS)
    wide = jnp.concatenate([jnp.roll(blocks, 1, 1)[:, :, COLS - 8:], blocks, jnp.roll(blocks, -1, 1)[:, :, :8]], 2)
    wide = jnp.pad(wide, ((0, 0), (0, 0), (0, LEV - COLS - 16)))
    seaw = wide.transpose(1, 0, 2)[:, :, None, :]
    coef = jnp.pad(jnp.where(land == 1, 0.5, 0.15).astype(f32), ((0, 0), (0, LEV - COLS)))[:, None, :]
    own, inv, ct, wave = consts
    vm = pl.BlockSpec(memory_space=pltpu.VMEM)
    hbm = pl.BlockSpec(memory_space=pl.ANY)
    dma = pltpu.SemaphoreType.DMA
    v = pltpu.VMEM
    air_out, sea_out = pl.pallas_call(
        functools.partial(kernel, nl),
        out_shape=(jax.ShapeDtypeStruct((ROWS, COLS, LEV), f32),
                   jax.ShapeDtypeStruct((nl, rp, 1, LEV), f32)),
        in_specs=[vm, vm, vm, vm, vm, pl.BlockSpec(memory_space=pltpu.SMEM), hbm, hbm, hbm, vm],
        out_specs=(vm, vm),
        scratch_shapes=[
            v((FRAMES, WIDE, LEV), f32), v((FRAMES, WIDE, LEV), f32),
            v((SPEC + 2, 2 * KW, LEV), f32), v((SPEC + 2, 2 * KW, LEV), f32),
            v((SPEC, 2 * KW, LEV), f32), v((nl, SPEC, ko, LEV), f32),
            v((STEPS - 1, nl, PACK, LEV), f32), v((STEPS - 1, PACK, LEV), f32),
            v((2, HALO, COLS, LEV), f32), v((2, HALO, 1, LEV), f32), v((2, HALO, 1, LEV), f32),
            v((ROWS, 1, LEV), f32), v((ROWS, 1, LEV), f32), v((nl, rp, 1, LEV), f32),
            v((2, FRAMES, 8, LEV), f32), v((2, FRAMES, 8, LEV), f32),
            v((2, 2 * KW, 96), bf16), v((2, QN, 2 * KW), bf16), v((2, 4, 2 * KW, nl * PACK), bf16),
            v((2, 2 * LEV, 2 * LEV), bf16), v((LEV, LEV), f32),
            v((QN, LEV), f32), v((QN, LEV), f32), v((144, LEV), f32), v((144, LEV), f32),
            v((QN, LEV), f32), v((2 * KW, LEV), f32), v((2, KW, LEV), f32),
            dma((3,)), dma((4,)), dma((4,)), dma((2,)), dma((4,)), dma((4,)), dma((2,)), dma((2,)),
            dma((STEPS - 1, 2)), dma((2,)),
        ],
        compiler_params=pltpu.CompilerParams(
            collective_id=0, has_side_effects=True, vmem_limit_bytes=56 * 1024 * 1024),
    )(air, seaw, coef, courant.reshape(1, LEV), vmix, cutoffs, own, inv, ct, wave)
    sea_out = sea_out[:, :, 0, :COLS].transpose(1, 0, 2).reshape(rp, nl * COLS)
    return air_out, sea_out


def solution(mesh):
    nl = mesh.shape["lon"]
    consts = tuple(jnp.asarray(x) for x in tables(nl))
    placed = (P("lat", "lon", None), P(("lat", "lon"), None), P("lat", "lon"), P(), P(), P())

    def run(*args):
        return jax.shard_map(
            functools.partial(local, nl),
            mesh=mesh,
            in_specs=((P(),) * 4,) + placed,
            out_specs=(P("lat", "lon", None), P(("lat", "lon"), None)),
            check_vma=False,
        )(consts, *args)

    return run
```

time: 2440 us -> 178 us (0.07)
  waiting for transfers between devices: 2060 us -> 0 us
  starting transfers between devices: 168 us -> 0 us
  Pallas kernels: 0 us -> 167 us
  local copies, waits for them, and re-layouts: 96.9 us -> 8.24 us
  matrix products: 57.8 us -> 0 us
  other arithmetic: 27.3 us -> 2.16 us
    psum x6 -> x0, waiting for transfers between devices: 1960 us -> none  [local(): real_part, imag_part = lax.psum((real_part, imag_part), 'lon')]
    pallas_call x0 -> x1, Pallas kernels: none -> 167 us  [local(): pl.pallas_call(functools.partial(kernel, nl), out_shape=(jax.ShapeDtypeSt...]
    all_to_all x12 -> x0, starting transfers between devices: 89.7 us -> none  [the longest x6 60.4 us: local(): lax.all_to_all(heat_flux, 'lon', split_axis=0, concat_axis=1, tiled=True)]
    ppermute x36 -> x0, starting transfers between devices: 78.2 us -> none  [the longest x18 60.6 us: with_halo(): after = lax.ppermute(leading, axis, down)]
    scatter-add x6 -> x0, local copies, waits for them, and re-layouts: 59.7 us -> none  [local(): air_temp = air_next.at[:, :, 0].add(air_gain * heat_flux)]
    dot_general x30 -> x0, matrix products: 57.8 us -> none  [the longest x6 14.9 us: inverse(): jnp.einsum('pkl,ck->pcl', real_part * weights, cosine, precision=lax.Prec...]
    ppermute x36 -> x0, waiting for transfers between devices: 53.9 us -> none  [the longest x18 47.5 us: with_halo(): before = lax.ppermute(last, axis, up)]
    all_to_all x12 -> x0, waiting for transfers between devices: 46 us -> none  [the longest x6 46 us: local(): lax.all_to_all(heat_flux, 'lon', split_axis=0, concat_axis=1, tiled=True)]
  transfers between devices with their start and end apart: 54 -> 0, of which waited for: 23 -> 0; matrix products, arithmetic and copies ran while one was open for 3% -> 0% of each run, Pallas kernels for 0% -> 0%
where the time goes in v1:
time: 178 us
  Pallas kernels  167 us (94%)
  local copies, waits for them, and re-layouts  8.24 us (5%)
  other arithmetic  2.16 us (1%)
    pallas_call x1, Pallas kernels, local(): pl.pallas_call(functools.partial(kernel, nl), out_shape=(jax.ShapeDtypeSt...  167 us
    unnamed x4, local copies, waits for them, and re-layouts  6.77 us

profile of v1, /device:TPU:0, one launch (start us, length us, event | category | flops | bytes accessed | tf_op | source)
XLA Modules:
  0.0 177.8 jit_solution(18300397341396610182)
XLA Ops:
  0.6 0.7 reduce
  1.4 0.1 reshape.10
  1.5 0.7 compare_select_fusion
  2.2 0.6 pad.9
  2.8 0.7 fusion
  3.5 3.4 %copy.12.a_ref = f32[32,90,128]{2,1,0:T(8,128)} copy(f32[32,90,128]{2,0,1:T(8,128)} %param.10) | data formatting | bytes 2949120 | tf_op args[0]
  6.9 166.8 %shard_map.113 = (f32[32,90,128]{2,1,0:T(8,128)}, f32[32,1,1,128]{3,2,1,0:T(1,128)}) custom-call(f32[32,90,128]{2,1,0:T(8,128)} %copy.12.a_ref, f32[32,1,1,128]{3,2,1,0:T(1,128)} %bitcast.4, f32[32,1,128]{2,1,0:T(1,128)} %bitcast.3, f32[1,128]{1,0:T(1,128)} %bitcast.5, f32[128,128]{1,0:T(8,128)} %vmix_ref.1, s32[32]{0:T(128)} %cut_ref.1, ...), custom_call_target="tpu_custom_call" | custom-call | tf_op jit(solution)/shard_map/pallas_call | solution.py:466
  173.7 0.0 copy-start
  173.7 3.4 %copy.13 = f32[32,90,128]{2,0,1:T(8,128)} copy(f32[32,90,128]{2,1,0:T(8,128)} %get-tuple-element.6) | data formatting | bytes 2949120
  177.1 0.0 copy-done
  177.1 0.7 reshape_transpose_squeeze.3
  (3 shorter events, 0.1 us)
Async XLA Ops:
  173.7 3.4 %copy-start = (f32[32,1,1,128]{3,2,1,0:T(1,128)S(1)}, f32[32,1,1,128]{3,2,1,0:T(1,128)}, u32[]{:S(2)}) copy-start(f32[32,1,1,128]{3,2,1,0:T(1,128)} %get-tuple-element.5) | copy-start | bytes 49156

commit v2 on v1

v2 whole, which is shorter than its diff:
```python
import functools

import jax
import jax.numpy as jnp
import ml_dtypes
import numpy as np
from jax import lax
from jax.experimental import pallas as pl
from jax.experimental.pallas import tpu as pltpu
from jax.sharding import PartitionSpec as P

STEPS = 6
NPOLE = 16
ROWS = 32
COLS = 90
KW = 128
LEV = 128
HALO = 6
FRAMES = 49
WIDE = 120
Q0, QN = 8, 104
SPEC = NPOLE + HALO
GROUPS, GW = 6, 16
STARTS = (0, 15, 30, 45, 60, 74)

f32, bf16 = jnp.float32, jnp.bfloat16
MESH = pl.DeviceIdType.MESH


def split(x):
    hi = x.astype(bf16)
    return hi, (x - hi.astype(f32)).astype(bf16)


def dot(a, b):
    return jnp.dot(a, b, preferred_element_type=f32)


def dot3(a, b):
    return dot(a[0], b[0]) + dot(a[1], b[0]) + dot(a[0], b[1])


def np_split(x):
    x = x.astype(np.float32)
    hi = x.astype(ml_dtypes.bfloat16)
    lo = (x - hi.astype(np.float32)).astype(ml_dtypes.bfloat16)
    return np.stack([hi, lo])


def tables(nl):
    nlon = nl * COLS
    kq = KW // nl
    k = (np.arange(nl)[:, None, None] * kq + np.arange(kq)[None, None, :]) * np.ones((1, 2, 1), int)
    sine = np.broadcast_to(np.arange(2)[None, :, None], k.shape).reshape(-1)
    k = k.reshape(-1)

    def fwd(c):
        ang = (c[..., None] * k % nlon) * (2.0 * np.pi / nlon)
        return np.where(sine == 0, np.cos(ang), np.sin(ang))

    d = np.arange(nl)[:, None]
    q = np.arange(QN)[None]
    weight = np.where(k == 0, 1.0, 2.0) / nlon
    inv = np.moveaxis(np_split(fwd((d * COLS + q - 8) % nlon) * weight), 0, 1)
    packed = []
    for g in range(GROUPS):
        c = STARTS[g] + np.arange(GW)[None]
        ours = np.logical_and(c >= g * 15, c < g * 15 + 15)
        packed.append(np.where(ours[..., None], fwd(d * COLS + c), 0.0).reshape(nl * GW, 2 * KW).T)
    fold = np.zeros((LEV, 2 * LEV))
    for g in range(GROUPS):
        for r in range(SPEC - 1):
            fold[21 * g + r, r + 8] = 0.5
            for near in (r - 1, r + 1):
                if near >= 0:
                    fold[21 * g + r, LEV + near + 8] = 0.5
    fold = np.concatenate([fold, fold]).astype(ml_dtypes.bfloat16)
    step = 2.0 * np.pi / nlon
    wave = np.stack([0.6 + 0.2 * np.cos(k * step), np.where(sine == 0, -1.0, 1.0) * np.sin(k * step)])
    wave = np.broadcast_to(wave[:, :, None], (2, 2 * KW, LEV)).astype(np.float32)
    return inv, np_split(np.concatenate(packed, 0)), fold, wave


def kernel(nl, a_ref, seaw_ref, coef_ref, cour_ref, vmix_ref, cut_ref, inv_hbm, ct_hbm, fold_ref,
           wave_ref, out_ref, seaout_ref, fa, fb, sa, sb, rowb, spec, ex, ep, ag, halo, coefr, sear,
           seab, seaf, seafin, sendx, recvx, inv, ct, vb, mt, a0t, coeft, st0, st1, fluxt,
           at, keept, tsem, asem, csem, seas, searow, xsem, rows, kss, exs, agsem, fins):
    lat, lon = lax.axis_index("lat"), lax.axis_index("lon")
    polar = jnp.logical_or(lat == 0, lat == 3)
    flip = lat == 3
    kq = KW // nl
    ko = 2 * kq
    rp = ROWS // nl
    half = nl // 2
    turn = lax.rem(lon, half) * 2 + lon // half
    lane = lax.broadcasted_iota(jnp.int32, (QN, LEV), 1)

    def natural(m):
        return jnp.where(flip, ROWS - 1 - m, m)

    def peers(body):
        def one(i, carry):
            body(lax.rem(lon + i, nl))
            return carry
        lax.fori_loop(1, nl, one, 0)

    def wait_bytes(ref, sem):
        pltpu.make_async_copy(ref, ref, sem).wait()

    def to_lon(src, dst, ssem, rsem, peer):
        return pltpu.make_async_remote_copy(src, dst, ssem, rsem, device_id={"lon": peer},
                                            device_id_type=MESH)

    loads = [
        pltpu.make_async_copy(inv_hbm.at[lon], inv, tsem.at[0]),
        pltpu.make_async_copy(ct_hbm, ct, tsem.at[1]),
    ]

    @pl.when(polar)
    def _():
        for load in loads:
            load.start()

    barrier = pltpu.get_barrier_semaphore()
    peers(lambda p: pl.semaphore_signal(barrier, inc=1, device_id={"lon": p}, device_id_type=MESH))

    @pl.when(lat < 3)
    def _():
        pl.semaphore_signal(barrier, inc=1, device_id={"lat": lat + 1}, device_id_type=MESH)

    @pl.when(lat > 0)
    def _():
        pl.semaphore_signal(barrier, inc=1, device_id={"lat": lat - 1}, device_id_type=MESH)

    pl.semaphore_wait(barrier, nl - 1 + jnp.where(polar, 1, 2))

    side = jnp.where(lat == 2, 1, 0)

    def lat_sends(src_ref, dst_ref, sems):
        def make(src, s, i, which, to):
            return pltpu.make_async_remote_copy(
                src_ref.at[src], dst_ref.at[s, i], sems.at[which], sems.at[2 + s],
                device_id={"lat": to}, device_id_type=MESH)

        @pl.when(lat < 3)
        def _():
            for i in range(HALO):
                make(jnp.where(lat == 2, ROWS - 1 - i, ROWS - HALO + i), side, i, 0, lat + 1).start()

        @pl.when(lat > 0)
        def _():
            for i in range(HALO):
                make(i, 1, i, 1, lat - 1).start()

    def lat_recvs(dst_ref, sems):
        wait_bytes(dst_ref.at[1], sems.at[3])

        @pl.when(jnp.logical_not(polar))
        def _():
            wait_bytes(dst_ref.at[0], sems.at[2])

    def lat_sent(dst_ref, sems):
        @pl.when(lat < 3)
        def _():
            wait_bytes(dst_ref.at[0], sems.at[0])

        @pl.when(lat > 0)
        def _():
            wait_bytes(dst_ref.at[0], sems.at[1])

    def owner(r):
        return (r % nl) % 2 * half + r % nl // 2

    @pl.when(polar)
    def _():
        for r in range(SPEC):
            @pl.when(lon != owner(r))
            def _():
                to_lon(a_ref.at[natural(r)], rowb.at[r // nl, lon], rows.at[0], rows.at[1 + r // nl], owner(r)).start()

    peers(lambda p: to_lon(seaw_ref.at[p], seab.at[pl.ds(rp * lon, rp)], seas.at[0], seas.at[1], p).start())
    lat_sends(coef_ref, coefr, csem)
    lat_sends(a_ref, halo, asem)

    @pl.when(polar)
    def _():
        for r in range(SPEC):
            @pl.when(lon == owner(r))
            def _():
                rowb[r // nl, lon] = a_ref[natural(r)]

    def own_sea(i, carry):
        seab[rp * lon + i] = seaw_ref[lon, i]
        return carry
    lax.fori_loop(0, rp, own_sea, 0)

    def clear(f, carry):
        z = jnp.zeros((8, LEV), f32)
        fa[f, pl.ds(0, 8), :] = z
        fa[f, pl.ds(WIDE - 16, 8), :] = z
        fa[f, pl.ds(WIDE - 8, 8), :] = z
        fb[f, pl.ds(0, 8), :] = z
        fb[f, pl.ds(WIDE - 8, 8), :] = z
        return carry
    lax.fori_loop(0, FRAMES, clear, 0)
    for f in (0, 1, 46, 47):
        fa[f] = jnp.zeros((WIDE, LEV), f32)
        fb[f] = jnp.zeros((WIDE, LEV), f32)
    fa[48] = jnp.zeros((WIDE, LEV), f32)
    fb[48] = jnp.zeros((WIDE, LEV), f32)

    def fill(m, carry):
        fa[m + 8, pl.ds(16, COLS), :] = a_ref[natural(m)]
        return carry
    lax.fori_loop(0, ROWS, fill, 0)

    col0 = jnp.broadcast_to(vmix_ref[:, 0:1], (LEV, LEV))
    rowid = lax.broadcasted_iota(jnp.int32, (LEV, LEV), 0)
    both = jnp.concatenate([vmix_ref[...], col0 + jnp.where(rowid == 0, 1.0, 0.0)], 1)
    bhi, blo = split(both)
    vb[0, pl.ds(0, LEV), :] = bhi
    vb[0, pl.ds(LEV, LEV), :] = bhi
    vb[1, pl.ds(0, LEV), :] = blo
    vb[1, pl.ds(LEV, LEV), :] = jnp.zeros_like(blo)

    def levels(x):
        both = jnp.concatenate(split(x), 1)
        res = dot(both, vb[0]) + dot(both, vb[1])
        return x + res[:, :LEV], res[:, LEV:]

    cour = cour_ref[...]
    east = 0.1 - 0.5 * cour
    west = 0.1 + 0.5 * cour
    lane1 = lax.broadcasted_iota(jnp.int32, (1, LEV), 1)
    vrow0 = vmix_ref[0:1, :] + jnp.where(lane1 == 0, 1.0, 0.0)
    half0 = jnp.where(lane1 == 0, 0.5, 0.0)
    kown = lon * kq + lax.rem(lax.broadcasted_iota(jnp.int32, (ko, LEV), 0), kq)
    olane = lax.broadcasted_iota(jnp.int32, (ko, LEV), 1)
    krow = lax.broadcasted_iota(jnp.int32, (2 * KW, LEV), 0)
    klane = lax.broadcasted_iota(jnp.int32, (2 * KW, LEV), 1)

    def swap(x, rowid):
        return jnp.where(lax.rem(rowid, ko) < kq, pltpu.roll(x, x.shape[0] - kq, 0), pltpu.roll(x, kq, 0))

    def cutoff(r):
        return cut_ref[jnp.where(flip, 2 * NPOLE - 1 - r, r)]

    mine = pl.ds(pl.multiple_of(lon * ko, 8), ko)

    @pl.when(polar)
    def _():
        cuts = jnp.full((1, LEV), KW, jnp.int32)
        for r in range(NPOLE):
            cuts = jnp.where(lane1 == r + 8, cutoff(r), cuts)
        kid = krow // ko * kq + lax.rem(krow, kq)
        keept[...] = jnp.where(kid <= cuts, 1.0, 0.0)
        for buf in (sa, sb):
            buf[0] = jnp.zeros((ko, LEV), f32)
            buf[SPEC + 1] = jnp.zeros((ko, LEV), f32)

    lat_recvs(halo, asem)
    for i in range(HALO):
        fa[40 + i, pl.ds(16, COLS), :] = halo[1, i]

    @pl.when(jnp.logical_not(polar))
    def _():
        for i in range(HALO):
            fa[2 + i, pl.ds(16, COLS), :] = halo[0, i]

    @pl.when(polar)
    def _():
        for i in range(HALO):
            fa[2 + i] = jnp.zeros((WIDE, LEV), f32)
            fb[2 + i] = jnp.zeros((WIDE, LEV), f32)

    def gather_rows(own_of, got):
        mt[...] = jnp.zeros_like(mt)

        def put(m, carry):
            mt[pl.ds(m + 8, 1), :] = own_of(m)
            return carry
        lax.fori_loop(0, ROWS, put, 0)
        for i in range(HALO):
            mt[40 + i:41 + i, :] = got[1, i]

        @pl.when(jnp.logical_not(polar))
        def _():
            for i in range(HALO):
                mt[2 + i:3 + i, :] = got[0, i]
        return mt[...].T

    lat_recvs(coefr, csem)
    fa[48, pl.ds(16, COLS), :] = gather_rows(lambda m: coef_ref[natural(m)], coefr)[:COLS]

    def pack(f, carry):
        sendx[0, f] = fa[f, pl.ds(16 + COLS - 8, 8), :]
        sendx[1, f] = fa[f, pl.ds(16, 8), :]
        return carry
    lax.fori_loop(2, FRAMES, pack, 0)
    zero = jnp.zeros((8, LEV), f32)
    for s in range(2):
        for f in range(2):
            sendx[s, f] = zero
    ahead = lax.rem(lon + 1, nl)
    behind = lax.rem(lon + nl - 1, nl)
    to_east = to_lon(sendx.at[0], recvx.at[0], xsem.at[0], xsem.at[2], ahead)
    to_west = to_lon(sendx.at[1], recvx.at[1], xsem.at[1], xsem.at[3], behind)
    to_east.start()
    to_west.start()

    wait_bytes(seab.at[pl.ds(0, ROWS - rp)], seas.at[1])
    lat_sends(seab, sear, searow)

    @pl.when(polar)
    def _():
        loads[0].wait()
        loads[1].wait()
        for slot in range(-(-SPEC // nl)):
            r = slot * nl + turn

            @pl.when(r < SPEC)
            def _():
                wait_bytes(rowb.at[slot, pl.ds(0, nl - 1)], rows.at[1 + slot])
                acc = jnp.zeros((2 * KW, LEV), f32)
                for g in range(GROUPS):
                    cols = rowb[slot, :, pl.ds(STARTS[g], GW), :].reshape(nl * GW, LEV)
                    tab = (ct[0, pl.ds(2 * KW * g, 2 * KW), :], ct[1, pl.ds(2 * KW * g, 2 * KW), :])
                    acc = acc + dot3(tab, split(cols))
                spec[slot] = acc

                def chunk(p):
                    return spec.at[slot, pl.ds(pl.multiple_of(p * ko, 8), ko)]
                peers(lambda p: to_lon(chunk(p), sa.at[r + 1], kss.at[0], kss.at[1], p).start())
                sa[r + 1] = spec[slot, mine, :]

    lat_recvs(sear, searow)
    st0[...] = jnp.zeros_like(st0)
    st1[...] = jnp.zeros_like(st1)
    st0[pl.ds(Q0, QN), :] = gather_rows(lambda m: seab[natural(m)], sear)[:QN]

    to_east.wait_recv()
    to_west.wait_recv()

    def unpack(f, carry):
        fa[f, pl.ds(8, 8), :] = recvx[0, f]
        fa[f, pl.ds(16 + COLS, 8), :] = recvx[1, f]
        return carry
    lax.fori_loop(2, FRAMES, unpack, 0)
    coeft[...] = fa[48, pl.ds(Q0, QN), :]

    def evolve(t, src, dst):
        wc = wave_ref[0, mine, :]
        ws = wave_ref[1, mine, :] * cour
        adv = []
        for r in range(SPEC - 1 - t):
            here = src[r + 1]
            x = wc * here + ws * swap(here, lax.broadcasted_iota(jnp.int32, (ko, LEV), 0)) + 0.1 * (src[r] + src[r + 2])
            adv.append(jnp.where(kown <= cutoff(r), x, 0.0) if r < NPOLE else x)
        new, low = levels(jnp.concatenate(adv, 0))
        level0 = jnp.zeros((ko, LEV), f32)
        for r in range(SPEC - 1 - t):
            dst[r + 1] = new[r * ko:(r + 1) * ko]
            if r < NPOLE:
                level0 = jnp.where(olane == r + 8, low[r * ko:(r + 1) * ko], level0)
        ep[t, pl.ds(0, ko), :] = level0
        ep[t, pl.ds(ko, ko), :] = new[(NPOLE - 1) * ko:NPOLE * ko]

    def message(t, height):
        part = pl.ds(0, height)
        ex[t, lon, part, :] = ep[t, part, :]
        peers(lambda p: to_lon(ep.at[t, part], ex.at[t, lon, part], exs.at[t, 0], exs.at[t, 1], p).start())

    def message_wait(t, height, which):
        wait_bytes(ex.at[t, pl.ds(0, nl - 1), pl.ds(0, height)], exs.at[t, which])

    def height(t):
        return 2 * ko + (GW if t else 0)

    @pl.when(polar)
    def _():
        extra = turn < SPEC % nl

        @pl.when(extra)
        def _():
            wait_bytes(sa.at[pl.ds(1, SPEC - SPEC // nl - 1)], kss.at[1])

        @pl.when(jnp.logical_not(extra))
        def _():
            wait_bytes(sa.at[pl.ds(1, SPEC - SPEC // nl)], kss.at[1])
        evolve(0, sa, sb)
        message(0, height(0))

    lane_ok = jnp.logical_or(lane >= 8, jnp.logical_not(polar))
    glane = lax.broadcasted_iota(jnp.int32, (GW, LEV), 1) // 21

    for t in range(1, STEPS + 1):
        src, dst = (fa, fb) if t % 2 else (fb, fa)
        sprev, snow = (sa, sb) if t % 2 else (sb, sa)
        sea, sea_next = (st0, st1) if t % 2 else (st1, st0)
        first = jnp.where(polar, 8 + NPOLE, 2 + t)
        count = jnp.where(polar, -(-(22 - t) // 4), -(-(44 - 2 * t) // 4))

        def grid_rows(i, acc):
            adv = []
            for j in range(4):
                f = first + 4 * i + j
                mid = pl.ds(Q0, QN)
                adv.append(0.6 * src[f, mid, :] + 0.1 * (src[f - 1, mid, :] + src[f + 1, mid, :])
                           + east * src[f, pl.ds(Q0 + 1, QN), :] + west * src[f, pl.ds(Q0 - 1, QN), :])
            new, low = levels(jnp.concatenate(adv, 0))
            for j in range(4):
                f = first + 4 * i + j
                dst[f, pl.ds(Q0, QN), :] = new[j * QN:(j + 1) * QN]
                acc = jnp.where(lane == f, low[j * QN:(j + 1) * QN], acc)
            return acc
        a0t[...] = lax.fori_loop(0, count, grid_rows, jnp.zeros((QN, LEV), f32))

        @pl.when(polar)
        def _():
            message_wait(t - 1, height(t - 1), 1)
            level0 = ex[t - 1, :, pl.ds(0, ko), :].reshape(2 * KW, LEV)
            edge = ex[t - 1, :, pl.ds(ko, ko), :].reshape(2 * KW, LEV)
            if t > 1:
                got = split(ex[t - 1, :, pl.ds(2 * ko, GW), :].reshape(nl * GW, LEV))
                res = jnp.zeros((2 * KW, LEV), f32)
                for g in range(GROUPS):
                    tab = (ct[0, pl.ds(2 * KW * g, 2 * KW), :], ct[1, pl.ds(2 * KW * g, 2 * KW), :])
                    res = jnp.where(klane // 21 == g, dot3(tab, got), res)
                hats = dot(jnp.concatenate(split(res), 1), fold_ref[...])
                hat, near = hats[:, :LEV], hats[:, LEV:]
                add = wave_ref[0] * hat + wave_ref[1] * cour[:, 0:1] * swap(hat, krow) + 0.1 * near
                add = add * keept[...]
                level0 = level0 + vrow0[:, 0:1] * add
                if t < STEPS:
                    at[...] = add
                    edge = edge + add[:, 7 + NPOLE:8 + NPOLE] * vrow0
                    own = at[mine, :]
                    for r in range(SPEC - t):
                        snow[r + 1] = snow[r + 1] + own[:, r + 8:r + 9] * vrow0
                else:
                    edge = add
            res = dot3((inv[0], inv[1]), split(jnp.concatenate([level0, edge], 1)))
            filtered = jnp.logical_and(lane >= 8, lane < 8 + NPOLE)
            a0t[...] = jnp.where(filtered, res[:, :LEV], a0t[...])
            if t < STEPS:
                dst[7 + NPOLE, pl.ds(Q0, QN), :] = res[:, LEV:]
                evolve(t, snow, sprev)
            else:
                at[pl.ds(0, QN), :] = res[:, LEV:]

        now = sea[pl.ds(Q0, QN), :]
        flux = coeft[...] * (now - a0t[...])
        fluxt[...] = flux
        around = (pltpu.roll(now, 1, 1) + pltpu.roll(now, LEV - 1, 1)
                  + sea[pl.ds(Q0 - 1, QN), :] + sea[pl.ds(Q0 + 1, QN), :])
        later = now - 0.3 * flux + 0.2 * (around - 4.0 * now)
        sea_next[pl.ds(Q0, QN), :] = jnp.where(lane_ok, later, 0.0)

        if t < STEPS:
            @pl.when(polar)
            def _():
                msg = jnp.zeros((GW, LEV), f32)
                for g in range(GROUPS):
                    turned = pltpu.roll(fluxt[pl.ds(8 + STARTS[g], GW), :], (21 * g - 8) % LEV, 1)
                    msg = jnp.where(glane == g, turned, msg)
                ep[t, pl.ds(2 * ko, GW), :] = msg
                message(t, height(t))
                if t == STEPS - 1:
                    whole = sprev.at[pl.ds(1, NPOLE)]
                    peers(lambda p: to_lon(whole, ag.at[lon], agsem.at[0], agsem.at[1], p).start())
                    ag[lon] = sprev[pl.ds(1, NPOLE)]

        def warm(f):
            dst[f, pl.ds(Q0, QN), :] = dst[f, pl.ds(Q0, QN), :] + flux[:, f:f + 1] * half0

        @pl.when(jnp.logical_not(polar))
        def _():
            for f in range(2 + t, 7 + NPOLE):
                warm(f)
        for f in range(7 + NPOLE, 46 - t):
            warm(f)

    last, sea = fa, st0

    mt[...] = sea[pl.ds(16, LEV), :].T

    def put_row(n, carry):
        seaf[n] = mt[pl.ds(natural(n) + 8, 1), :]
        return carry
    lax.fori_loop(0, ROWS, put_row, 0)
    peers(lambda p: to_lon(seaf.at[pl.ds(rp * p, rp)], seafin.at[lon], fins.at[0], fins.at[1], p).start())

    def own_fin(i, carry):
        seafin[lon, i] = seaf[rp * lon + i]
        return carry
    lax.fori_loop(0, rp, own_fin, 0)

    def give_grid(m, carry):
        out_ref[natural(m)] = last[m + 8, pl.ds(16, COLS), :]
        return carry
    lax.fori_loop(jnp.where(polar, NPOLE, 0), ROWS, give_grid, 0)

    @pl.when(polar)
    def _():
        wait_bytes(ag.at[pl.ds(0, nl - 1)], agsem.at[1])
        tab = (inv[0], inv[1])
        for i in range(NPOLE // 2):
            pair = jnp.concatenate([ag[:, 2 * i].reshape(2 * KW, LEV), ag[:, 2 * i + 1].reshape(2 * KW, LEV)], 1)
            res = dot3(tab, split(pair))
            for j in range(2):
                r = 2 * i + j
                value = (res[:, j * LEV:(j + 1) * LEV] + at[pl.ds(0, QN), r + 8:r + 9] * vrow0
                         + fluxt[:, r + 8:r + 9] * half0)
                out_ref[natural(r)] = value[8:8 + COLS]

    wait_bytes(seafin.at[pl.ds(0, nl - 1)], fins.at[1])
    seaout_ref[...] = seafin[...]

    wait_bytes(seafin.at[pl.ds(0, nl - 1)], fins.at[0])
    wait_bytes(seab.at[pl.ds(0, ROWS - rp)], seas.at[0])
    lat_sent(halo, asem)
    lat_sent(coefr, csem)
    lat_sent(sear, searow)
    to_east.wait_send()
    to_west.wait_send()

    @pl.when(polar)
    def _():
        for r in range(SPEC):
            @pl.when(lon != owner(r))
            def _():
                wait_bytes(a_ref.at[0], rows.at[0])
        for slot in range(-(-SPEC // nl)):
            @pl.when(slot * nl + turn < SPEC)
            def _():
                wait_bytes(spec.at[slot, pl.ds(0, (nl - 1) * ko)], kss.at[0])
        for t in range(STEPS):
            message_wait(t, height(t), 0)
        wait_bytes(ag.at[pl.ds(0, nl - 1)], agsem.at[0])


def local(nl, consts, air, sea, land, courant, vmix, cutoffs):
    rp = ROWS // nl
    ko = 2 * KW // nl
    blocks = sea.reshape(rp, nl, COLS)
    wide = jnp.concatenate([jnp.roll(blocks, 1, 1)[:, :, COLS - 8:], blocks, jnp.roll(blocks, -1, 1)[:, :, :8]], 2)
    wide = jnp.pad(wide, ((0, 0), (0, 0), (0, LEV - COLS - 16)))
    seaw = wide.transpose(1, 0, 2)[:, :, None, :]
    coef = jnp.pad(jnp.where(land == 1, 0.5, 0.15).astype(f32), ((0, 0), (0, LEV - COLS)))[:, None, :]
    inv, ct, fold, wave = consts
    slots = -(-SPEC // nl)
    vm = pl.BlockSpec(memory_space=pltpu.VMEM)
    hbm = pl.BlockSpec(memory_space=pl.ANY)
    dma = pltpu.SemaphoreType.DMA
    v = pltpu.VMEM
    air_out, sea_out = pl.pallas_call(
        functools.partial(kernel, nl),
        out_shape=(jax.ShapeDtypeStruct((ROWS, COLS, LEV), f32),
                   jax.ShapeDtypeStruct((nl, rp, 1, LEV), f32)),
        in_specs=[vm, vm, vm, vm, vm, pl.BlockSpec(memory_space=pltpu.SMEM), hbm, hbm, vm, vm],
        out_specs=(vm, vm),
        scratch_shapes=[
            v((FRAMES, WIDE, LEV), f32), v((FRAMES, WIDE, LEV), f32),
            v((SPEC + 2, ko, LEV), f32), v((SPEC + 2, ko, LEV), f32),
            v((slots, nl, COLS, LEV), f32), v((slots, 2 * KW, LEV), f32),
            v((STEPS, nl, 2 * ko + GW, LEV), f32), v((STEPS, 2 * ko + GW, LEV), f32),
            v((nl, NPOLE, ko, LEV), f32),
            v((2, HALO, COLS, LEV), f32), v((2, HALO, 1, LEV), f32), v((2, HALO, 1, LEV), f32),
            v((ROWS, 1, LEV), f32), v((ROWS, 1, LEV), f32), v((nl, rp, 1, LEV), f32),
            v((2, FRAMES, 8, LEV), f32), v((2, FRAMES, 8, LEV), f32),
            v((2, QN, 2 * KW), bf16), v((2, GROUPS * 2 * KW, nl * GW), bf16),
            v((2, 2 * LEV, 2 * LEV), bf16), v((LEV, LEV), f32),
            v((QN, LEV), f32), v((QN, LEV), f32), v((144, LEV), f32), v((144, LEV), f32),
            v((QN, LEV), f32), v((2 * KW, LEV), f32), v((2 * KW, LEV), f32),
            dma((2,)), dma((4,)), dma((4,)), dma((2,)), dma((4,)), dma((4,)), dma((1 + slots,)), dma((2,)),
            dma((STEPS, 2)), dma((2,)), dma((2,)),
        ],
        compiler_params=pltpu.CompilerParams(
            collective_id=0, has_side_effects=True, vmem_limit_bytes=56 * 1024 * 1024),
    )(air, seaw, coef, courant.reshape(1, LEV), vmix, cutoffs, inv, ct, fold, wave)
    sea_out = sea_out[:, :, 0, :COLS].transpose(1, 0, 2).reshape(rp, nl * COLS)
    return air_out, sea_out


def solution(mesh):
    nl = mesh.shape["lon"]
    consts = tuple(jnp.asarray(x) for x in tables(nl))
    placed = (P("lat", "lon", None), P(("lat", "lon"), None), P("lat", "lon"), P(), P(), P())

    def run(*args):
        return jax.shard_map(
            functools.partial(local, nl),
            mesh=mesh,
            in_specs=((P(),) * 4,) + placed,
            out_specs=(P("lat", "lon", None), P(("lat", "lon"), None)),
            check_vma=False,
        )(consts, *args)

    return run
```

time: 178 us -> 120 us (0.67); the launches traced: 178 us -> 118 us
  Pallas kernels: 167 us -> 107 us
    pallas_call x1, Pallas kernels: 167 us -> 107 us  [local(): pl.pallas_call(functools.partial(kernel, nl), out_shape=(jax.ShapeDtypeSt...]
where the time goes in v2:
time: 120 us; the launch traced here: 118 us
  Pallas kernels  107 us (89%)
  local copies, waits for them, and re-layouts  8.24 us (7%)
  other arithmetic  2.16 us (2%)
    pallas_call x1, Pallas kernels, local(): pl.pallas_call(functools.partial(kernel, nl), out_shape=(jax.ShapeDtypeSt...  107 us
    unnamed x4, local copies, waits for them, and re-layouts  6.77 us

profile of v2, /device:TPU:0, one launch (start us, length us, event | category | flops | bytes accessed | tf_op | source)
XLA Modules:
  0.0 117.7 jit_solution(3131685994798204409)
XLA Ops:
  0.6 0.7 reduce
  1.4 0.1 reshape.10
  1.5 0.7 compare_select_fusion
  2.2 0.6 pad.9
  2.8 0.7 fusion
  3.5 3.4 %copy.12.a_ref = f32[32,90,128]{2,1,0:T(8,128)} copy(f32[32,90,128]{2,0,1:T(8,128)} %param.10) | data formatting | bytes 2949120 | tf_op args[0]
  6.9 106.6 %shard_map.113 = (f32[32,90,128]{2,1,0:T(8,128)}, f32[32,1,1,128]{3,2,1,0:T(1,128)}) custom-call(f32[32,90,128]{2,1,0:T(8,128)} %copy.12.a_ref, f32[32,1,1,128]{3,2,1,0:T(1,128)} %bitcast.4, f32[32,1,128]{2,1,0:T(1,128)} %bitcast.3, f32[1,128]{1,0:T(1,128)} %bitcast.5, f32[128,128]{1,0:T(8,128)} %vmix_ref.1, s32[32]{0:T(128)} %cut_ref.1, ...), custom_call_target="tpu_custom_call" | custom-call | tf_op jit(solution)/shard_map/pallas_call | solution.py:556
  113.5 0.0 copy-start
  113.5 3.4 %copy.13 = f32[32,90,128]{2,0,1:T(8,128)} copy(f32[32,90,128]{2,1,0:T(8,128)} %get-tuple-element.6) | data formatting | bytes 2949120
  116.9 0.0 copy-done
  117.0 0.7 reshape_transpose_squeeze.3
  (3 shorter events, 0.1 us)
Async XLA Ops:
  113.5 3.4 %copy-start = (f32[32,1,1,128]{3,2,1,0:T(1,128)S(1)}, f32[32,1,1,128]{3,2,1,0:T(1,128)}, u32[]{:S(2)}) copy-start(f32[32,1,1,128]{3,2,1,0:T(1,128)} %get-tuple-element.5) | copy-start | bytes 49156

commit v3 on v2

--- a/solution.py
+++ b/solution.py
@@ -40,6 +40,12 @@
     return dot(a[0], b[0]) + dot(a[1], b[0]) + dot(a[0], b[1])
 
 
+def dot3n(a, b):
+    n = b[0].shape[1]
+    both = dot(a[0], jnp.concatenate(b, 1))
+    return both[:, :n] + both[:, n:] + dot(a[1], b[0])
+
+
 def np_split(x):
     x = x.astype(np.float32)
     hi = x.astype(ml_dtypes.bfloat16)
@@ -62,6 +68,7 @@
     q = np.arange(QN)[None]
     weight = np.where(k == 0, 1.0, 2.0) / nlon
     inv = np.moveaxis(np_split(fwd((d * COLS + q - 8) % nlon) * weight), 0, 1)
+    everywhere = np_split(fwd(np.arange(nl * COLS).reshape(nl, COLS)) * weight)
     packed = []
     for g in range(GROUPS):
         c = STARTS[g] + np.arange(GW)[None]
@@ -78,13 +85,13 @@
     step = 2.0 * np.pi / nlon
     wave = np.stack([0.6 + 0.2 * np.cos(k * step), np.where(sine == 0, -1.0, 1.0) * np.sin(k * step)])
     wave = np.broadcast_to(wave[:, :, None], (2, 2 * KW, LEV)).astype(np.float32)
-    return inv, np_split(np.concatenate(packed, 0)), fold, wave
-
-
-def kernel(nl, a_ref, seaw_ref, coef_ref, cour_ref, vmix_ref, cut_ref, inv_hbm, ct_hbm, fold_ref,
-           wave_ref, out_ref, seaout_ref, fa, fb, sa, sb, rowb, spec, ex, ep, ag, halo, coefr, sear,
-           seab, seaf, seafin, sendx, recvx, inv, ct, vb, mt, a0t, coeft, st0, st1, fluxt,
-           at, keept, tsem, asem, csem, seas, searow, xsem, rows, kss, exs, agsem, fins):
+    return inv, everywhere, np_split(np.concatenate(packed, 0)), fold, wave
+
+
+def kernel(nl, a_ref, seaw_ref, coef_ref, cour_ref, vmix_ref, cut_ref, inv_hbm, all_hbm, ct_hbm, fold_ref,
+           wave_ref, out_ref, seaout_ref, fa, fb, sa, sb, rowb, spec, fx, fp, ex, ep, rs6, stage, fin, xs, xr, halo, coefr, sear,
+           seab, seaf, seafin, sendx, recvx, inv, inva, ct, vb, mt, a0t, coeft, st0, st1, fluxt,
+           at, keept, tsem, asem, csem, seas, searow, xsem, rows, kss, fxs, exs, r6, fsem, xss, fins):
     lat, lon = lax.axis_index("lat"), lax.axis_index("lon")
     polar = jnp.logical_or(lat == 0, lat == 3)
     flip = lat == 3
@@ -114,6 +121,7 @@
     loads = [
         pltpu.make_async_copy(inv_hbm.at[lon], inv, tsem.at[0]),
         pltpu.make_async_copy(ct_hbm, ct, tsem.at[1]),
+        pltpu.make_async_copy(all_hbm, inva, tsem.at[2]),
     ]
 
     @pl.when(polar)
@@ -311,10 +319,15 @@
     wait_bytes(seab.at[pl.ds(0, ROWS - rp)], seas.at[1])
     lat_sends(seab, sear, searow)
 
+    def across(u, x):
+        return lax.dot_general(u, x, (((1,), (1,)), ((), ())), preferred_element_type=f32)
+
     @pl.when(polar)
     def _():
         loads[0].wait()
         loads[1].wait()
+        ident = jnp.where(rowid == lax.broadcasted_iota(jnp.int32, (LEV, LEV), 1), 1.0, 0.0)
+        ucol = split((vmix_ref[...] + ident).T[0:8, :])
         for slot in range(-(-SPEC // nl)):
             r = slot * nl + turn
 
@@ -325,8 +338,15 @@
                 for g in range(GROUPS):
                     cols = rowb[slot, :, pl.ds(STARTS[g], GW), :].reshape(nl * GW, LEV)
                     tab = (ct[0, pl.ds(2 * KW * g, 2 * KW), :], ct[1, pl.ds(2 * KW * g, 2 * KW), :])
-                    acc = acc + dot3(tab, split(cols))
+                    acc = acc + dot3n(tab, split(cols))
                 spec[slot] = acc
+                waved = wave_ref[0] * acc + wave_ref[1] * cour * swap(acc, krow)
+                pair = split(jnp.concatenate([waved, acc], 0))
+                low = across(ucol[0], pair[0]) + across(ucol[1], pair[0]) + across(ucol[0], pair[1])
+                for i in range(4):
+                    xs[slot, i:i + 1, :] = low[0:1, i * LEV:(i + 1) * LEV]
+                    xr[r, i:i + 1, :] = low[0:1, i * LEV:(i + 1) * LEV]
+                peers(lambda p: to_lon(xs.at[slot], xr.at[r], xss.at[0], xss.at[1], p).start())
 
                 def chunk(p):
                     return spec.at[slot, pl.ds(pl.multiple_of(p * ko, 8), ko)]
@@ -365,30 +385,51 @@
         ep[t, pl.ds(0, ko), :] = level0
         ep[t, pl.ds(ko, ko), :] = new[(NPOLE - 1) * ko:NPOLE * ko]
 
-    def message(t, height):
-        part = pl.ds(0, height)
-        ex[t, lon, part, :] = ep[t, part, :]
-        peers(lambda p: to_lon(ep.at[t, part], ex.at[t, lon, part], exs.at[t, 0], exs.at[t, 1], p).start())
-
-    def message_wait(t, height, which):
-        wait_bytes(ex.at[t, pl.ds(0, nl - 1), pl.ds(0, height)], exs.at[t, which])
-
-    def height(t):
-        return 2 * ko + (GW if t else 0)
-
-    @pl.when(polar)
-    def _():
-        extra = turn < SPEC % nl
-
+    def message(got, made, sems, t):
+        got[t, lon] = made[t]
+        peers(lambda p: to_lon(made.at[t], got.at[t, lon], sems.at[t, 0], sems.at[t, 1], p).start())
+
+    def message_wait(got, sems, t, which):
+        wait_bytes(got.at[t, pl.ds(0, nl - 1)], sems.at[t, which])
+
+    extra = turn < SPEC % nl
+
+    def others_rows(ref, sem):
         @pl.when(extra)
         def _():
-            wait_bytes(sa.at[pl.ds(1, SPEC - SPEC // nl - 1)], kss.at[1])
+            wait_bytes(ref.at[pl.ds(0, SPEC - SPEC // nl - 1)], sem)
 
         @pl.when(jnp.logical_not(extra))
         def _():
-            wait_bytes(sa.at[pl.ds(1, SPEC - SPEC // nl)], kss.at[1])
-        evolve(0, sa, sb)
-        message(0, height(0))
+            wait_bytes(ref.at[pl.ds(0, SPEC - SPEC // nl)], sem)
+
+    def first_level0():
+        others_rows(xr, xss.at[1])
+        mt[...] = jnp.zeros_like(mt)
+        cols = []
+        for i in range(4):
+            for r in range(NPOLE + 1):
+                mt[r + 8:r + 9, :] = xr[r, i:i + 1, :]
+            cols.append(mt[...].T)
+        own, beside = jnp.concatenate(cols[:2], 0), jnp.concatenate(cols[2:], 0)
+        near = pltpu.roll(beside, 1, 1) + pltpu.roll(beside, LEV - 1, 1)
+        return (own + 0.1 * near) * keept[...]
+
+    def last_rows():
+        loads[2].wait()
+        for slot in range(-(-NPOLE // nl)):
+            r = slot * nl + turn
+
+            @pl.when(r < NPOLE)
+            def _():
+                wait_bytes(rs6.at[slot, pl.ds(0, nl - 1)], r6.at[1 + slot])
+                waves = split(rs6[slot].reshape(2 * KW, LEV))
+                fin[r] = dot3n((inva[0, lon], inva[1, lon]), waves)
+
+                def one(p):
+                    stage[slot, p] = dot3n((inva[0, p], inva[1, p]), waves)
+                    to_lon(stage.at[slot, p], fin.at[r], fsem.at[0], fsem.at[1], p).start()
+                peers(one)
 
     lane_ok = jnp.logical_or(lane >= 8, jnp.logical_not(polar))
     glane = lax.broadcasted_iota(jnp.int32, (GW, LEV), 1) // 21
@@ -417,58 +458,79 @@
 
         @pl.when(polar)
         def _():
-            message_wait(t - 1, height(t - 1), 1)
-            level0 = ex[t - 1, :, pl.ds(0, ko), :].reshape(2 * KW, LEV)
-            edge = ex[t - 1, :, pl.ds(ko, ko), :].reshape(2 * KW, LEV)
+            if t == STEPS:
+                last_rows()
             if t > 1:
-                got = split(ex[t - 1, :, pl.ds(2 * ko, GW), :].reshape(nl * GW, LEV))
+                message_wait(fx, fxs, t - 1, 1)
+                got = split(fx[t - 1].reshape(nl * GW, LEV))
                 res = jnp.zeros((2 * KW, LEV), f32)
                 for g in range(GROUPS):
                     tab = (ct[0, pl.ds(2 * KW * g, 2 * KW), :], ct[1, pl.ds(2 * KW * g, 2 * KW), :])
-                    res = jnp.where(klane // 21 == g, dot3(tab, got), res)
+                    res = jnp.where(klane // 21 == g, dot3n(tab, got), res)
                 hats = dot(jnp.concatenate(split(res), 1), fold_ref[...])
                 hat, near = hats[:, :LEV], hats[:, LEV:]
                 add = wave_ref[0] * hat + wave_ref[1] * cour[:, 0:1] * swap(hat, krow) + 0.1 * near
                 add = add * keept[...]
-                level0 = level0 + vrow0[:, 0:1] * add
-                if t < STEPS:
-                    at[...] = add
-                    edge = edge + add[:, 7 + NPOLE:8 + NPOLE] * vrow0
+                at[...] = add
+            if t == 1:
+                res = dot3n((inv[0], inv[1]), split(first_level0()))
+            else:
+                message_wait(ex, exs, t - 1, 1)
+                level0 = ex[t - 1, :, pl.ds(0, ko), :].reshape(2 * KW, LEV) + vrow0[:, 0:1] * add
+                edge = ex[t - 1, :, pl.ds(ko, ko), :].reshape(2 * KW, LEV)
+                edge = edge + add[:, 7 + NPOLE:8 + NPOLE] * vrow0 if t < STEPS else add
+                res = dot3((inv[0], inv[1]), split(jnp.concatenate([level0, edge], 1)))
+            filtered = jnp.logical_and(lane >= 8, lane < 8 + NPOLE)
+            a0t[...] = jnp.where(filtered, res[:, :LEV], a0t[...])
+            if t == STEPS:
+                at[pl.ds(0, QN), :] = res[:, LEV:]
+            elif t > 1:
+                dst[7 + NPOLE, pl.ds(Q0, QN), :] = res[:, LEV:]
+
+        now = sea[pl.ds(Q0, QN), :]
+        flux = coeft[...] * (now - a0t[...])
+        fluxt[...] = flux
+
+        if t < STEPS:
+            @pl.when(polar)
+            def _():
+                msg = jnp.zeros((GW, LEV), f32)
+                for g in range(GROUPS):
+                    turned = pltpu.roll(fluxt[pl.ds(8 + STARTS[g], GW), :], (21 * g - 8) % LEV, 1)
+                    msg = jnp.where(glane == g, turned, msg)
+                fp[t] = msg
+                message(fx, fp, fxs, t)
+                if t == 1:
+                    others_rows(sa, kss.at[1])
+                    evolve(0, sa, sb)
+                    message(ex, ep, exs, 0)
+                else:
                     own = at[mine, :]
                     for r in range(SPEC - t):
                         snow[r + 1] = snow[r + 1] + own[:, r + 8:r + 9] * vrow0
-                else:
-                    edge = add
-            res = dot3((inv[0], inv[1]), split(jnp.concatenate([level0, edge], 1)))
-            filtered = jnp.logical_and(lane >= 8, lane < 8 + NPOLE)
-            a0t[...] = jnp.where(filtered, res[:, :LEV], a0t[...])
-            if t < STEPS:
-                dst[7 + NPOLE, pl.ds(Q0, QN), :] = res[:, LEV:]
                 evolve(t, snow, sprev)
-            else:
-                at[pl.ds(0, QN), :] = res[:, LEV:]
-
-        now = sea[pl.ds(Q0, QN), :]
-        flux = coeft[...] * (now - a0t[...])
-        fluxt[...] = flux
+                message(ex, ep, exs, t)
+                if t == STEPS - 1:
+                    for r in range(NPOLE):
+                        @pl.when(lon != owner(r))
+                        def _():
+                            to_lon(sprev.at[r + 1], rs6.at[r // nl, lon], r6.at[0], r6.at[1 + r // nl], owner(r)).start()
+
+                        @pl.when(lon == owner(r))
+                        def _():
+                            rs6[r // nl, lon] = sprev[r + 1]
+
         around = (pltpu.roll(now, 1, 1) + pltpu.roll(now, LEV - 1, 1)
                   + sea[pl.ds(Q0 - 1, QN), :] + sea[pl.ds(Q0 + 1, QN), :])
         later = now - 0.3 * flux + 0.2 * (around - 4.0 * now)
         sea_next[pl.ds(Q0, QN), :] = jnp.where(lane_ok, later, 0.0)
 
-        if t < STEPS:
+        if t == 1:
             @pl.when(polar)
             def _():
-                msg = jnp.zeros((GW, LEV), f32)
-                for g in range(GROUPS):
-                    turned = pltpu.roll(fluxt[pl.ds(8 + STARTS[g], GW), :], (21 * g - 8) % LEV, 1)
-                    msg = jnp.where(glane == g, turned, msg)
-                ep[t, pl.ds(2 * ko, GW), :] = msg
-                message(t, height(t))
-                if t == STEPS - 1:
-                    whole = sprev.at[pl.ds(1, NPOLE)]
-                    peers(lambda p: to_lon(whole, ag.at[lon], agsem.at[0], agsem.at[1], p).start())
-                    ag[lon] = sprev[pl.ds(1, NPOLE)]
+                message_wait(ex, exs, 0, 1)
+                edge = ex[0, :, pl.ds(ko, ko), :].reshape(2 * KW, LEV)
+                dst[7 + NPOLE, pl.ds(Q0, QN), :] = dot3n((inv[0], inv[1]), split(edge))
 
         def warm(f):
             dst[f, pl.ds(Q0, QN), :] = dst[f, pl.ds(Q0, QN), :] + flux[:, f:f + 1] * half0
@@ -502,16 +564,18 @@
 
     @pl.when(polar)
     def _():
-        wait_bytes(ag.at[pl.ds(0, nl - 1)], agsem.at[1])
-        tab = (inv[0], inv[1])
-        for i in range(NPOLE // 2):
-            pair = jnp.concatenate([ag[:, 2 * i].reshape(2 * KW, LEV), ag[:, 2 * i + 1].reshape(2 * KW, LEV)], 1)
-            res = dot3(tab, split(pair))
-            for j in range(2):
-                r = 2 * i + j
-                value = (res[:, j * LEV:(j + 1) * LEV] + at[pl.ds(0, QN), r + 8:r + 9] * vrow0
-                         + fluxt[:, r + 8:r + 9] * half0)
-                out_ref[natural(r)] = value[8:8 + COLS]
+        more = turn < NPOLE % nl
+
+        @pl.when(more)
+        def _():
+            wait_bytes(fin.at[pl.ds(0, NPOLE - NPOLE // nl - 1)], fsem.at[1])
+
+        @pl.when(jnp.logical_not(more))
+        def _():
+            wait_bytes(fin.at[pl.ds(0, NPOLE - NPOLE // nl)], fsem.at[1])
+        for r in range(NPOLE):
+            out_ref[natural(r)] = (fin[r] + at[pl.ds(8, COLS), r + 8:r + 9] * vrow0
+                                   + fluxt[pl.ds(8, COLS), r + 8:r + 9] * half0)
 
     wait_bytes(seafin.at[pl.ds(0, nl - 1)], fins.at[1])
     seaout_ref[...] = seafin[...]
@@ -534,9 +598,19 @@
             @pl.when(slot * nl + turn < SPEC)
             def _():
                 wait_bytes(spec.at[slot, pl.ds(0, (nl - 1) * ko)], kss.at[0])
+                peers(lambda p: wait_bytes(xs.at[slot], xss.at[0]))
         for t in range(STEPS):
-            message_wait(t, height(t), 0)
-        wait_bytes(ag.at[pl.ds(0, nl - 1)], agsem.at[0])
+            message_wait(ex, exs, t, 0)
+        for t in range(1, STEPS):
+            message_wait(fx, fxs, t, 0)
+        for r in range(NPOLE):
+            @pl.when(lon != owner(r))
+            def _():
+                wait_bytes(sa.at[0], r6.at[0])
+        for slot in range(-(-NPOLE // nl)):
+            @pl.when(slot * nl + turn < NPOLE)
+            def _():
+                wait_bytes(stage.at[slot, pl.ds(0, nl - 1)], fsem.at[0])
 
 
 def local(nl, consts, air, sea, land, courant, vmix, cutoffs):
@@ -547,7 +621,8 @@
     wide = jnp.pad(wide, ((0, 0), (0, 0), (0, LEV - COLS - 16)))
     seaw = wide.transpose(1, 0, 2)[:, :, None, :]
     coef = jnp.pad(jnp.where(land == 1, 0.5, 0.15).astype(f32), ((0, 0), (0, LEV - COLS)))[:, None, :]
-    inv, ct, fold, wave = consts
+    inv, inva, ct, fold, wave = consts
+    last = -(-NPOLE // nl)
     slots = -(-SPEC // nl)
     vm = pl.BlockSpec(memory_space=pltpu.VMEM)
     hbm = pl.BlockSpec(memory_space=pl.ANY)
@@ -557,27 +632,29 @@
         functools.partial(kernel, nl),
         out_shape=(jax.ShapeDtypeStruct((ROWS, COLS, LEV), f32),
                    jax.ShapeDtypeStruct((nl, rp, 1, LEV), f32)),
-        in_specs=[vm, vm, vm, vm, vm, pl.BlockSpec(memory_space=pltpu.SMEM), hbm, hbm, vm, vm],
+        in_specs=[vm, vm, vm, vm, vm, pl.BlockSpec(memory_space=pltpu.SMEM), hbm, hbm, hbm, vm, vm],
         out_specs=(vm, vm),
         scratch_shapes=[
             v((FRAMES, WIDE, LEV), f32), v((FRAMES, WIDE, LEV), f32),
             v((SPEC + 2, ko, LEV), f32), v((SPEC + 2, ko, LEV), f32),
             v((slots, nl, COLS, LEV), f32), v((slots, 2 * KW, LEV), f32),
-            v((STEPS, nl, 2 * ko + GW, LEV), f32), v((STEPS, 2 * ko + GW, LEV), f32),
-            v((nl, NPOLE, ko, LEV), f32),
+            v((STEPS, nl, GW, LEV), f32), v((STEPS, GW, LEV), f32),
+            v((STEPS, nl, 2 * ko, LEV), f32), v((STEPS, 2 * ko, LEV), f32),
+            v((last, nl, ko, LEV), f32), v((last, nl, COLS, LEV), f32), v((NPOLE, COLS, LEV), f32),
+            v((slots, 4, LEV), f32), v((SPEC, 4, LEV), f32),
             v((2, HALO, COLS, LEV), f32), v((2, HALO, 1, LEV), f32), v((2, HALO, 1, LEV), f32),
             v((ROWS, 1, LEV), f32), v((ROWS, 1, LEV), f32), v((nl, rp, 1, LEV), f32),
             v((2, FRAMES, 8, LEV), f32), v((2, FRAMES, 8, LEV), f32),
-            v((2, QN, 2 * KW), bf16), v((2, GROUPS * 2 * KW, nl * GW), bf16),
+            v((2, QN, 2 * KW), bf16), v((2, nl, COLS, 2 * KW), bf16), v((2, GROUPS * 2 * KW, nl * GW), bf16),
             v((2, 2 * LEV, 2 * LEV), bf16), v((LEV, LEV), f32),
             v((QN, LEV), f32), v((QN, LEV), f32), v((144, LEV), f32), v((144, LEV), f32),
             v((QN, LEV), f32), v((2 * KW, LEV), f32), v((2 * KW, LEV), f32),
-            dma((2,)), dma((4,)), dma((4,)), dma((2,)), dma((4,)), dma((4,)), dma((1 + slots,)), dma((2,)),
-            dma((STEPS, 2)), dma((2,)), dma((2,)),
+            dma((3,)), dma((4,)), dma((4,)), dma((2,)), dma((4,)), dma((4,)), dma((1 + slots,)), dma((2,)),
+            dma((STEPS, 2)), dma((STEPS, 2)), dma((1 + last,)), dma((2,)), dma((2,)), dma((2,)),
         ],
         compiler_params=pltpu.CompilerParams(
             collective_id=0, has_side_effects=True, vmem_limit_bytes=56 * 1024 * 1024),
-    )(air, seaw, coef, courant.reshape(1, LEV), vmix, cutoffs, inv, ct, fold, wave)
+    )(air, seaw, coef, courant.reshape(1, LEV), vmix, cutoffs, inv, inva, ct, fold, wave)
     sea_out = sea_out[:, :, 0, :COLS].transpose(1, 0, 2).reshape(rp, nl * COLS)
     return air_out, sea_out
 
@@ -591,7 +668,7 @@
         return jax.shard_map(
             functools.partial(local, nl),
             mesh=mesh,
-            in_specs=((P(),) * 4,) + placed,
+            in_specs=((P(),) * 5,) + placed,
             out_specs=(P("lat", "lon", None), P(("lat", "lon"), None)),
             check_vma=False,
         )(consts, *args)

time: 120 us -> 110 us (0.917)
  Pallas kernels: 107 us -> 97.7 us
    pallas_call x1, Pallas kernels: 107 us -> 97.7 us  [local(): pl.pallas_call(functools.partial(kernel, nl), out_shape=(jax.ShapeDtypeSt...]
where the time goes in v3:
time: 110 us; the launch traced here: 109 us
  Pallas kernels  97.7 us (89%)
  local copies, waits for them, and re-layouts  8.24 us (7%)
  other arithmetic  2.16 us (2%)
    pallas_call x1, Pallas kernels, local(): pl.pallas_call(functools.partial(kernel, nl), out_shape=(jax.ShapeDtypeSt...  97.7 us
    unnamed x4, local copies, waits for them, and re-layouts  6.77 us

profile of v3, /device:TPU:0, one launch (start us, length us, event | category | flops | bytes accessed | tf_op | source)
XLA Modules:
  0.0 108.7 jit_solution(3056537291024406896)
XLA Ops:
  0.6 0.7 reduce
  1.4 0.1 reshape.10
  1.5 0.7 compare_select_fusion
  2.2 0.6 pad.9
  2.8 0.7 fusion
  3.5 3.4 %copy.13.a_ref = f32[32,90,128]{2,1,0:T(8,128)} copy(f32[32,90,128]{2,0,1:T(8,128)} %param.11) | data formatting | bytes 2949120 | tf_op args[0]
  6.9 97.7 %shard_map.122 = (f32[32,90,128]{2,1,0:T(8,128)}, f32[32,1,1,128]{3,2,1,0:T(1,128)}) custom-call(f32[32,90,128]{2,1,0:T(8,128)} %copy.13.a_ref, f32[32,1,1,128]{3,2,1,0:T(1,128)} %bitcast.4, f32[32,1,128]{2,1,0:T(1,128)} %bitcast.3, f32[1,128]{1,0:T(1,128)} %bitcast.5, f32[128,128]{1,0:T(8,128)} %vmix_ref.1, s32[32]{0:T(128)} %cut_ref.1, ...), custom_call_target="tpu_custom_call" | custom-call | tf_op jit(solution)/shard_map/pallas_call | solution.py:631
  104.6 0.0 copy-start
  104.6 3.4 %copy.14 = f32[32,90,128]{2,0,1:T(8,128)} copy(f32[32,90,128]{2,1,0:T(8,128)} %get-tuple-element.6) | data formatting | bytes 2949120
  107.9 0.0 copy-done
  108.0 0.7 reshape_transpose_squeeze.3
  (3 shorter events, 0.1 us)
Async XLA Ops:
  104.6 3.4 %copy-start = (f32[32,1,1,128]{3,2,1,0:T(1,128)S(1)}, f32[32,1,1,128]{3,2,1,0:T(1,128)}, u32[]{:S(2)}) copy-start(f32[32,1,1,128]{3,2,1,0:T(1,128)} %get-tuple-element.5) | copy-start | bytes 49156

commit v4 on v3

--- a/solution.py
+++ b/solution.py
@@ -88,10 +88,10 @@
     return inv, everywhere, np_split(np.concatenate(packed, 0)), fold, wave
 
 
-def kernel(nl, a_ref, seaw_ref, coef_ref, cour_ref, vmix_ref, cut_ref, inv_hbm, all_hbm, ct_hbm, fold_ref,
-           wave_ref, out_ref, seaout_ref, fa, fb, sa, sb, rowb, spec, fx, fp, ex, ep, rs6, stage, fin, xs, xr, halo, coefr, sear,
+def kernel(nl, a_hbm, seaw_ref, land_ref, cour_ref, vmix_ref, cut_ref, inv_hbm, all_hbm, ct_hbm, fold_ref,
+           wave_ref, out_hbm, seaout_ref, a_ref, out_ref, coef_ref, fa, fb, sa, sb, rowb, spec, fx, fp, ex, ep, rs6, stage, fin, xs, xr, halo, coefr, sear,
            seab, seaf, seafin, sendx, recvx, inv, inva, ct, vb, mt, a0t, coeft, st0, st1, fluxt,
-           at, keept, tsem, asem, csem, seas, searow, xsem, rows, kss, fxs, exs, r6, fsem, xss, fins):
+           at, keept, tsem, asem, csem, seas, searow, xsem, rows, kss, fxs, exs, r6, fsem, xss, fins, isem, osem):
     lat, lon = lax.axis_index("lat"), lax.axis_index("lon")
     polar = jnp.logical_or(lat == 0, lat == 3)
     flip = lat == 3
@@ -129,6 +129,10 @@
         for load in loads:
             load.start()
 
+    rows_in = [pltpu.make_async_copy(a_hbm.at[:, m, :], a_ref.at[m], isem) for m in range(ROWS)]
+    for row in rows_in:
+        row.start()
+
     barrier = pltpu.get_barrier_semaphore()
     peers(lambda p: pl.semaphore_signal(barrier, inc=1, device_id={"lon": p}, device_id_type=MESH))
 
@@ -141,6 +145,13 @@
         pl.semaphore_signal(barrier, inc=1, device_id={"lat": lat - 1}, device_id_type=MESH)
 
     pl.semaphore_wait(barrier, nl - 1 + jnp.where(polar, 1, 2))
+
+    def own_coef(m, carry):
+        coef_ref[m] = jnp.zeros((1, LEV), f32)
+        coef_ref[m, :, pl.ds(0, COLS)] = jnp.where(land_ref[pl.ds(m, 1), :] == 1, 0.5, 0.15)
+        return carry
+    lax.fori_loop(0, ROWS, own_coef, 0)
+    wait_bytes(a_ref, isem)
 
     side = jnp.where(lat == 2, 1, 0)
 
@@ -417,19 +428,21 @@
 
     def last_rows():
         loads[2].wait()
-        for slot in range(-(-NPOLE // nl)):
-            r = slot * nl + turn
-
-            @pl.when(r < NPOLE)
-            def _():
-                wait_bytes(rs6.at[slot, pl.ds(0, nl - 1)], r6.at[1 + slot])
-                waves = split(rs6[slot].reshape(2 * KW, LEV))
-                fin[r] = dot3n((inva[0, lon], inva[1, lon]), waves)
-
-                def one(p):
-                    stage[slot, p] = dot3n((inva[0, p], inva[1, p]), waves)
-                    to_lon(stage.at[slot, p], fin.at[r], fsem.at[0], fsem.at[1], p).start()
-                peers(one)
+        here = lax.rem(lon, half)
+        base = lon - here
+        for slot in range(NPOLE // half):
+            r = slot * half + here
+            wait_bytes(rs6.at[slot, pl.ds(0, nl - 1)], r6.at[1 + slot])
+            waves = split(rs6[slot].reshape(2 * KW, LEV))
+
+            def one(i, carry):
+                at_i = lax.rem(here + i, half)
+                p = base + at_i
+                stage[slot, at_i] = dot3n((inva[0, p], inva[1, p]), waves)
+                to_lon(stage.at[slot, at_i], fin.at[r], fsem.at[0], fsem.at[1], p).start()
+                return carry
+            lax.fori_loop(1, half, one, 0)
+            fin[r] = dot3n((inva[0, lon], inva[1, lon]), waves)
 
     lane_ok = jnp.logical_or(lane >= 8, jnp.logical_not(polar))
     glane = lax.broadcasted_iota(jnp.int32, (GW, LEV), 1) // 21
@@ -512,13 +525,14 @@
                 message(ex, ep, exs, t)
                 if t == STEPS - 1:
                     for r in range(NPOLE):
-                        @pl.when(lon != owner(r))
-                        def _():
-                            to_lon(sprev.at[r + 1], rs6.at[r // nl, lon], r6.at[0], r6.at[1 + r // nl], owner(r)).start()
-
-                        @pl.when(lon == owner(r))
-                        def _():
-                            rs6[r // nl, lon] = sprev[r + 1]
+                        for dev in (r % half, half + r % half):
+                            @pl.when(lon != dev)
+                            def _():
+                                to_lon(sprev.at[r + 1], rs6.at[r // half, lon], r6.at[0], r6.at[1 + r // half], dev).start()
+
+                            @pl.when(lon == dev)
+                            def _():
+                                rs6[r // half, lon] = sprev[r + 1]
 
         around = (pltpu.roll(now, 1, 1) + pltpu.roll(now, LEV - 1, 1)
                   + sea[pl.ds(Q0 - 1, QN), :] + sea[pl.ds(Q0 + 1, QN), :])
@@ -533,14 +547,17 @@
                 dst[7 + NPOLE, pl.ds(Q0, QN), :] = dot3n((inv[0], inv[1]), split(edge))
 
         def warm(f):
-            dst[f, pl.ds(Q0, QN), :] = dst[f, pl.ds(Q0, QN), :] + flux[:, f:f + 1] * half0
-
-        @pl.when(jnp.logical_not(polar))
-        def _():
-            for f in range(2 + t, 7 + NPOLE):
+            dst[f, pl.ds(Q0, QN), :] = dst[f, pl.ds(Q0, QN), :] + fluxt[:, f:f + 1] * half0
+
+        def warm_all():
+            @pl.when(jnp.logical_not(polar))
+            def _():
+                for f in range(2 + t, 7 + NPOLE):
+                    warm(f)
+            for f in range(7 + NPOLE, 46 - t):
                 warm(f)
-        for f in range(7 + NPOLE, 46 - t):
-            warm(f)
+        if t < STEPS:
+            warm_all()
 
     last, sea = fa, st0
 
@@ -557,29 +574,37 @@
         return carry
     lax.fori_loop(0, rp, own_fin, 0)
 
+    warm_all()
+
     def give_grid(m, carry):
         out_ref[natural(m)] = last[m + 8, pl.ds(16, COLS), :]
         return carry
     lax.fori_loop(jnp.where(polar, NPOLE, 0), ROWS, give_grid, 0)
 
+    def row_out(m):
+        n = natural(m)
+        pltpu.make_async_copy(out_ref.at[n], out_hbm.at[:, n, :], osem).start()
+
+    for m in range(NPOLE, ROWS):
+        row_out(m)
+
+    @pl.when(jnp.logical_not(polar))
+    def _():
+        for m in range(NPOLE):
+            row_out(m)
+
     @pl.when(polar)
     def _():
-        more = turn < NPOLE % nl
-
-        @pl.when(more)
-        def _():
-            wait_bytes(fin.at[pl.ds(0, NPOLE - NPOLE // nl - 1)], fsem.at[1])
-
-        @pl.when(jnp.logical_not(more))
-        def _():
-            wait_bytes(fin.at[pl.ds(0, NPOLE - NPOLE // nl)], fsem.at[1])
+        wait_bytes(fin.at[pl.ds(0, NPOLE - NPOLE // half)], fsem.at[1])
         for r in range(NPOLE):
             out_ref[natural(r)] = (fin[r] + at[pl.ds(8, COLS), r + 8:r + 9] * vrow0
                                    + fluxt[pl.ds(8, COLS), r + 8:r + 9] * half0)
+            row_out(r)
 
     wait_bytes(seafin.at[pl.ds(0, nl - 1)], fins.at[1])
     seaout_ref[...] = seafin[...]
 
+    wait_bytes(out_ref, osem)
     wait_bytes(seafin.at[pl.ds(0, nl - 1)], fins.at[0])
     wait_bytes(seab.at[pl.ds(0, ROWS - rp)], seas.at[0])
     lat_sent(halo, asem)
@@ -604,13 +629,12 @@
         for t in range(1, STEPS):
             message_wait(fx, fxs, t, 0)
         for r in range(NPOLE):
-            @pl.when(lon != owner(r))
-            def _():
-                wait_bytes(sa.at[0], r6.at[0])
-        for slot in range(-(-NPOLE // nl)):
-            @pl.when(slot * nl + turn < NPOLE)
-            def _():
-                wait_bytes(stage.at[slot, pl.ds(0, nl - 1)], fsem.at[0])
+            for dev in (r % half, half + r % half):
+                @pl.when(lon != dev)
+                def _():
+                    wait_bytes(sa.at[0], r6.at[0])
+        for slot in range(NPOLE // half):
+            wait_bytes(stage.at[slot, pl.ds(0, half - 1)], fsem.at[0])
 
 
 def local(nl, consts, air, sea, land, courant, vmix, cutoffs):
@@ -620,9 +644,9 @@
     wide = jnp.concatenate([jnp.roll(blocks, 1, 1)[:, :, COLS - 8:], blocks, jnp.roll(blocks, -1, 1)[:, :, :8]], 2)
     wide = jnp.pad(wide, ((0, 0), (0, 0), (0, LEV - COLS - 16)))
     seaw = wide.transpose(1, 0, 2)[:, :, None, :]
-    coef = jnp.pad(jnp.where(land == 1, 0.5, 0.15).astype(f32), ((0, 0), (0, LEV - COLS)))[:, None, :]
     inv, inva, ct, fold, wave = consts
-    last = -(-NPOLE // nl)
+    half = nl // 2
+    last = NPOLE // half
     slots = -(-SPEC // nl)
     vm = pl.BlockSpec(memory_space=pltpu.VMEM)
     hbm = pl.BlockSpec(memory_space=pl.ANY)
@@ -630,17 +654,18 @@
     v = pltpu.VMEM
     air_out, sea_out = pl.pallas_call(
         functools.partial(kernel, nl),
-        out_shape=(jax.ShapeDtypeStruct((ROWS, COLS, LEV), f32),
+        out_shape=(jax.ShapeDtypeStruct((COLS, ROWS, LEV), f32),
                    jax.ShapeDtypeStruct((nl, rp, 1, LEV), f32)),
-        in_specs=[vm, vm, vm, vm, vm, pl.BlockSpec(memory_space=pltpu.SMEM), hbm, hbm, hbm, vm, vm],
-        out_specs=(vm, vm),
+        in_specs=[hbm, vm, vm, vm, vm, pl.BlockSpec(memory_space=pltpu.SMEM), hbm, hbm, hbm, vm, vm],
+        out_specs=(hbm, vm),
         scratch_shapes=[
+            v((ROWS, COLS, LEV), f32), v((ROWS, COLS, LEV), f32), v((ROWS, 1, LEV), f32),
             v((FRAMES, WIDE, LEV), f32), v((FRAMES, WIDE, LEV), f32),
             v((SPEC + 2, ko, LEV), f32), v((SPEC + 2, ko, LEV), f32),
             v((slots, nl, COLS, LEV), f32), v((slots, 2 * KW, LEV), f32),
             v((STEPS, nl, GW, LEV), f32), v((STEPS, GW, LEV), f32),
             v((STEPS, nl, 2 * ko, LEV), f32), v((STEPS, 2 * ko, LEV), f32),
-            v((last, nl, ko, LEV), f32), v((last, nl, COLS, LEV), f32), v((NPOLE, COLS, LEV), f32),
+            v((last, nl, ko, LEV), f32), v((last, half, COLS, LEV), f32), v((NPOLE, COLS, LEV), f32),
             v((slots, 4, LEV), f32), v((SPEC, 4, LEV), f32),
             v((2, HALO, COLS, LEV), f32), v((2, HALO, 1, LEV), f32), v((2, HALO, 1, LEV), f32),
             v((ROWS, 1, LEV), f32), v((ROWS, 1, LEV), f32), v((nl, rp, 1, LEV), f32),
@@ -650,13 +675,13 @@
             v((QN, LEV), f32), v((QN, LEV), f32), v((144, LEV), f32), v((144, LEV), f32),
             v((QN, LEV), f32), v((2 * KW, LEV), f32), v((2 * KW, LEV), f32),
             dma((3,)), dma((4,)), dma((4,)), dma((2,)), dma((4,)), dma((4,)), dma((1 + slots,)), dma((2,)),
-            dma((STEPS, 2)), dma((STEPS, 2)), dma((1 + last,)), dma((2,)), dma((2,)), dma((2,)),
+            dma((STEPS, 2)), dma((STEPS, 2)), dma((1 + last,)), dma((2,)), dma((2,)), dma((2,)), dma, dma,
         ],
         compiler_params=pltpu.CompilerParams(
             collective_id=0, has_side_effects=True, vmem_limit_bytes=56 * 1024 * 1024),
-    )(air, seaw, coef, courant.reshape(1, LEV), vmix, cutoffs, inv, inva, ct, fold, wave)
+    )(air.transpose(1, 0, 2), seaw, land, courant.reshape(1, LEV), vmix, cutoffs, inv, inva, ct, fold, wave)
     sea_out = sea_out[:, :, 0, :COLS].transpose(1, 0, 2).reshape(rp, nl * COLS)
-    return air_out, sea_out
+    return air_out.transpose(1, 0, 2), sea_out
 
 
 def solution(mesh):

time: 110 us -> 98.8 us (0.90)
  Pallas kernels: 97.7 us -> 92.2 us
  local copies, waits for them, and re-layouts: 8.24 us -> 4.18 us
    pallas_call x1, Pallas kernels: 97.7 us -> 92.2 us  [local(): pl.pallas_call(functools.partial(kernel, nl), out_shape=(jax.ShapeDtypeSt...]
    unnamed x4 -> x1, local copies, waits for them, and re-layouts: 6.77 us -> 2.59 us
where the time goes in v4:
time: 98.8 us; the launch traced here: 98.5 us
  Pallas kernels  92.2 us (93%)
  local copies, waits for them, and re-layouts  4.18 us (4%)
  other arithmetic  1.43 us (1%)
    pallas_call x1, Pallas kernels, local(): pl.pallas_call(functools.partial(kernel, nl), out_shape=(jax.ShapeDtypeSt...  92.2 us
    unnamed x1, local copies, waits for them, and re-layouts  2.59 us

profile of v4, /device:TPU:0, one launch (start us, length us, event | category | flops | bytes accessed | tf_op | source)
XLA Modules:
  0.0 98.5 jit_solution(16376445116581407006)
XLA Ops:
  0.6 0.7 reduce
  1.4 0.1 reshape.10
  1.5 0.7 fusion
  2.2 92.2 %shard_map.122 = (f32[90,32,128]{2,1,0:T(8,128)}, f32[32,1,1,128]{3,2,1,0:T(1,128)}) custom-call(f32[90,32,128]{2,1,0:T(8,128)} %bitcast.4, f32[32,1,1,128]{3,2,1,0:T(1,128)} %bitcast.6, s32[32,90]{1,0:T(8,128)} %land_ref.1, f32[1,128]{1,0:T(1,128)} %bitcast.7, f32[128,128]{1,0:T(8,128)} %vmix_ref.1, s32[32]{0:T(128)} %cut_ref.1, ...), custom_call_target="tpu_custom_call" | custom-call | tf_op jit(solution)/shard_map/pallas_call | solution.py:655
  94.4 0.8 slice_reduce_fusion
  95.1 0.7 reshape_transpose_squeeze.3
  95.9 2.6 %copy.14 = f32[32,90,128]{2,0,1:T(8,128)} copy(f32[32,90,128]{2,0,1:T(8,128)} %bitcast.5) | data formatting | bytes 2949120
  (2 shorter events, 0.0 us)

commit v5 on v4

--- a/solution.py
+++ b/solution.py
@@ -88,10 +88,10 @@
     return inv, everywhere, np_split(np.concatenate(packed, 0)), fold, wave
 
 
-def kernel(nl, a_hbm, seaw_ref, land_ref, cour_ref, vmix_ref, cut_ref, inv_hbm, all_hbm, ct_hbm, fold_ref,
-           wave_ref, out_hbm, seaout_ref, a_ref, out_ref, coef_ref, fa, fb, sa, sb, rowb, spec, fx, fp, ex, ep, rs6, stage, fin, xs, xr, halo, coefr, sear,
+def kernel(nl, a_hbm, sea_ref, land_ref, cour_ref, vmix_ref, cut_ref, inv_hbm, all_hbm, ct_hbm, fold_ref,
+           wave_ref, out_hbm, seaout_ref, a_ref, out_ref, coef_ref, seaw_ref, fa, fb, sa, sb, rowb, spec, fx, fp, ex, ep, rs6, stage, fin, xs, xr, halo, coefr, sear,
            seab, seaf, seafin, sendx, recvx, inv, inva, ct, vb, mt, a0t, coeft, st0, st1, fluxt,
-           at, keept, tsem, asem, csem, seas, searow, xsem, rows, kss, fxs, exs, r6, fsem, xss, fins, isem, osem):
+           at, keept, twice, vecs, tsem, asem, csem, seas, searow, xsem, rows, kss, fxs, exs, r6, fsem, xss, fins, isem, osem):
     lat, lon = lax.axis_index("lat"), lax.axis_index("lon")
     polar = jnp.logical_or(lat == 0, lat == 3)
     flip = lat == 3
@@ -106,10 +106,18 @@
         return jnp.where(flip, ROWS - 1 - m, m)
 
     def peers(body):
-        def one(i, carry):
-            body(lax.rem(lon + i, nl))
+        here = lax.rem(lon, half)
+        base = lon - here
+
+        def across_half(i, carry):
+            body(half - base + lax.rem(here + i, half))
             return carry
-        lax.fori_loop(1, nl, one, 0)
+
+        def beside(i, carry):
+            body(base + lax.rem(here + i, half))
+            return carry
+        lax.fori_loop(0, half, across_half, 0)
+        lax.fori_loop(1, half, beside, 0)
 
     def wait_bytes(ref, sem):
         pltpu.make_async_copy(ref, ref, sem).wait()
@@ -151,6 +159,20 @@
         coef_ref[m, :, pl.ds(0, COLS)] = jnp.where(land_ref[pl.ds(m, 1), :] == 1, 0.5, 0.15)
         return carry
     lax.fori_loop(0, ROWS, own_coef, 0)
+
+    nlon = nl * COLS
+    for d in range(nl):
+        for i in range(rp):
+            seaw_ref[d, i] = jnp.zeros((1, LEV), f32)
+            lo, hi = d * COLS - 8, d * COLS + COLS + 8
+            if lo < 0:
+                seaw_ref[d, i, :, 0:8] = sea_ref[i:i + 1, nlon - 8:nlon]
+                seaw_ref[d, i, :, 8:COLS + 16] = sea_ref[i:i + 1, 0:hi]
+            elif hi > nlon:
+                seaw_ref[d, i, :, 0:COLS + 8] = sea_ref[i:i + 1, lo:nlon]
+                seaw_ref[d, i, :, COLS + 8:COLS + 16] = sea_ref[i:i + 1, 0:8]
+            else:
+                seaw_ref[d, i, :, 0:COLS + 16] = sea_ref[i:i + 1, lo:hi]
     wait_bytes(a_ref, isem)
 
     side = jnp.where(lat == 2, 1, 0)
@@ -273,6 +295,8 @@
             cuts = jnp.where(lane1 == r + 8, cutoff(r), cuts)
         kid = krow // ko * kq + lax.rem(krow, kq)
         keept[...] = jnp.where(kid <= cuts, 1.0, 0.0)
+        pair = jnp.where(lax.broadcasted_iota(jnp.int32, (8, LEV), 0) == 0, 1.0, cour) * vrow0
+        vecs[...] = levels(pair)[0]
         for buf in (sa, sb):
             buf[0] = jnp.zeros((ko, LEV), f32)
             buf[SPEC + 1] = jnp.zeros((ko, LEV), f32)
@@ -379,22 +403,24 @@
     lax.fori_loop(2, FRAMES, unpack, 0)
     coeft[...] = fa[48, pl.ds(Q0, QN), :]
 
-    def evolve(t, src, dst):
+    def evolve(rows, src, dst, slot):
         wc = wave_ref[0, mine, :]
         ws = wave_ref[1, mine, :] * cour
         adv = []
-        for r in range(SPEC - 1 - t):
+        for r in range(rows):
             here = src[r + 1]
             x = wc * here + ws * swap(here, lax.broadcasted_iota(jnp.int32, (ko, LEV), 0)) + 0.1 * (src[r] + src[r + 2])
             adv.append(jnp.where(kown <= cutoff(r), x, 0.0) if r < NPOLE else x)
         new, low = levels(jnp.concatenate(adv, 0))
-        level0 = jnp.zeros((ko, LEV), f32)
-        for r in range(SPEC - 1 - t):
-            dst[r + 1] = new[r * ko:(r + 1) * ko]
-            if r < NPOLE:
+        if dst is not None:
+            for r in range(rows):
+                dst[r + 1] = new[r * ko:(r + 1) * ko]
+        if slot is not None:
+            level0 = jnp.zeros((ko, LEV), f32)
+            for r in range(NPOLE):
                 level0 = jnp.where(olane == r + 8, low[r * ko:(r + 1) * ko], level0)
-        ep[t, pl.ds(0, ko), :] = level0
-        ep[t, pl.ds(ko, ko), :] = new[(NPOLE - 1) * ko:NPOLE * ko]
+            ep[slot, pl.ds(0, ko), :] = level0
+            ep[slot, pl.ds(ko, ko), :] = new[(NPOLE - 1) * ko:NPOLE * ko]
 
     def message(got, made, sems, t):
         got[t, lon] = made[t]
@@ -491,6 +517,11 @@
                 message_wait(ex, exs, t - 1, 1)
                 level0 = ex[t - 1, :, pl.ds(0, ko), :].reshape(2 * KW, LEV) + vrow0[:, 0:1] * add
                 edge = ex[t - 1, :, pl.ds(ko, ko), :].reshape(2 * KW, LEV)
+                if t > 2:
+                    for i in range(2):
+                        vec = vecs[i:i + 1, :]
+                        level0 = level0 + vec[:, 0:1] * twice[i]
+                        edge = edge + twice[i][:, 7 + NPOLE:8 + NPOLE] * vec
                 edge = edge + add[:, 7 + NPOLE:8 + NPOLE] * vrow0 if t < STEPS else add
                 res = dot3((inv[0], inv[1]), split(jnp.concatenate([level0, edge], 1)))
             filtered = jnp.logical_and(lane >= 8, lane < 8 + NPOLE)
@@ -515,14 +546,23 @@
                 message(fx, fp, fxs, t)
                 if t == 1:
                     others_rows(sa, kss.at[1])
-                    evolve(0, sa, sb)
+                    evolve(SPEC - 1, sa, sb, 0)
                     message(ex, ep, exs, 0)
                 else:
                     own = at[mine, :]
                     for r in range(SPEC - t):
                         snow[r + 1] = snow[r + 1] + own[:, r + 8:r + 9] * vrow0
-                evolve(t, snow, sprev)
-                message(ex, ep, exs, t)
+                evolve(SPEC - 1 - t, snow, sprev, 1 if t == 1 else None)
+                if t == 1:
+                    message(ex, ep, exs, 1)
+                if t < STEPS - 1:
+                    evolve(NPOLE, sprev, None, t + 1)
+                    message(ex, ep, exs, t + 1)
+                if 1 < t:
+                    add = at[...]
+                    near = pltpu.roll(add, 1, 1) + pltpu.roll(add, LEV - 1, 1)
+                    twice[0] = (wave_ref[0] * add + 0.1 * near) * keept[...]
+                    twice[1] = wave_ref[1] * swap(add, krow) * keept[...]
                 if t == STEPS - 1:
                     for r in range(NPOLE):
                         for dev in (r % half, half + r % half):
@@ -602,7 +642,9 @@
             row_out(r)
 
     wait_bytes(seafin.at[pl.ds(0, nl - 1)], fins.at[1])
-    seaout_ref[...] = seafin[...]
+    for d in range(nl):
+        for i in range(rp):
+            seaout_ref[i:i + 1, d * COLS:d * COLS + COLS] = seafin[d, i, :, 0:COLS]
 
     wait_bytes(out_ref, osem)
     wait_bytes(seafin.at[pl.ds(0, nl - 1)], fins.at[0])
@@ -640,10 +682,6 @@
 def local(nl, consts, air, sea, land, courant, vmix, cutoffs):
     rp = ROWS // nl
     ko = 2 * KW // nl
-    blocks = sea.reshape(rp, nl, COLS)
-    wide = jnp.concatenate([jnp.roll(blocks, 1, 1)[:, :, COLS - 8:], blocks, jnp.roll(blocks, -1, 1)[:, :, :8]], 2)
-    wide = jnp.pad(wide, ((0, 0), (0, 0), (0, LEV - COLS - 16)))
-    seaw = wide.transpose(1, 0, 2)[:, :, None, :]
     inv, inva, ct, fold, wave = consts
     half = nl // 2
     last = NPOLE // half
@@ -655,11 +693,11 @@
     air_out, sea_out = pl.pallas_call(
         functools.partial(kernel, nl),
         out_shape=(jax.ShapeDtypeStruct((COLS, ROWS, LEV), f32),
-                   jax.ShapeDtypeStruct((nl, rp, 1, LEV), f32)),
+                   jax.ShapeDtypeStruct((rp, nl * COLS), f32)),
         in_specs=[hbm, vm, vm, vm, vm, pl.BlockSpec(memory_space=pltpu.SMEM), hbm, hbm, hbm, vm, vm],
         out_specs=(hbm, vm),
         scratch_shapes=[
-            v((ROWS, COLS, LEV), f32), v((ROWS, COLS, LEV), f32), v((ROWS, 1, LEV), f32),
+            v((ROWS, COLS, LEV), f32), v((ROWS, COLS, LEV), f32), v((ROWS, 1, LEV), f32), v((nl, rp, 1, LEV), f32),
             v((FRAMES, WIDE, LEV), f32), v((FRAMES, WIDE, LEV), f32),
             v((SPEC + 2, ko, LEV), f32), v((SPEC + 2, ko, LEV), f32),
             v((slots, nl, COLS, LEV), f32), v((slots, 2 * KW, LEV), f32),
@@ -673,14 +711,13 @@
             v((2, QN, 2 * KW), bf16), v((2, nl, COLS, 2 * KW), bf16), v((2, GROUPS * 2 * KW, nl * GW), bf16),
             v((2, 2 * LEV, 2 * LEV), bf16), v((LEV, LEV), f32),
             v((QN, LEV), f32), v((QN, LEV), f32), v((144, LEV), f32), v((144, LEV), f32),
-            v((QN, LEV), f32), v((2 * KW, LEV), f32), v((2 * KW, LEV), f32),
+            v((QN, LEV), f32), v((2 * KW, LEV), f32), v((2 * KW, LEV), f32), v((2, 2 * KW, LEV), f32), v((8, LEV), f32),
             dma((3,)), dma((4,)), dma((4,)), dma((2,)), dma((4,)), dma((4,)), dma((1 + slots,)), dma((2,)),
             dma((STEPS, 2)), dma((STEPS, 2)), dma((1 + last,)), dma((2,)), dma((2,)), dma((2,)), dma, dma,
         ],
         compiler_params=pltpu.CompilerParams(
             collective_id=0, has_side_effects=True, vmem_limit_bytes=56 * 1024 * 1024),
-    )(air.transpose(1, 0, 2), seaw, land, courant.reshape(1, LEV), vmix, cutoffs, inv, inva, ct, fold, wave)
-    sea_out = sea_out[:, :, 0, :COLS].transpose(1, 0, 2).reshape(rp, nl * COLS)
+    )(air.transpose(1, 0, 2), sea, land, courant.reshape(1, LEV), vmix, cutoffs, inv, inva, ct, fold, wave)
     return air_out.transpose(1, 0, 2), sea_out
 
 

time: 98.8 us -> 95.4 us (0.966)
  Pallas kernels: 92.2 us -> 90.6 us
  other arithmetic: 1.43 us -> 0 us
    pallas_call x1, Pallas kernels: 92.2 us -> 90.6 us  [local(): pl.pallas_call(functools.partial(kernel, nl), out_shape=(jax.ShapeDtypeSt...]
    unnamed x1 -> x2, local copies, waits for them, and re-layouts: 2.59 us -> 3.9 us
where the time goes in v5:
time: 95.4 us; the launch traced here: 95.2 us
  Pallas kernels  90.6 us (95%)
  local copies, waits for them, and re-layouts  3.9 us (4%)
    pallas_call x1, Pallas kernels, local(): pl.pallas_call(functools.partial(kernel, nl), out_shape=(jax.ShapeDtypeSt...  90.6 us
    unnamed x2, local copies, waits for them, and re-layouts  3.9 us

profile of v5, /device:TPU:0, one launch (start us, length us, event | category | flops | bytes accessed | tf_op | source)
XLA Modules:
  0.0 95.2 jit_solution(13412273855831217072)
XLA Ops:
  0.6 90.6 %shard_map.122 = (f32[90,32,128]{2,1,0:T(8,128)}, f32[1,2880]{1,0:T(1,128)}) custom-call(f32[90,32,128]{2,1,0:T(8,128)} %bitcast.3, f32[1,2880]{1,0:T(1,128)} %sea_ref.1, s32[32,90]{1,0:T(8,128)} %land_ref.1, f32[1,128]{1,0:T(1,128)} %bitcast.5, f32[128,128]{1,0:T(8,128)} %vmix_ref.1, s32[32]{0:T(128)} %cut_ref.1, ...), custom_call_target="tpu_custom_call" | custom-call | tf_op jit(solution)/shard_map/pallas_call | solution.py:693
  91.3 2.6 %copy.15 = f32[32,90,128]{2,0,1:T(8,128)} copy(f32[32,90,128]{2,0,1:T(8,128)} %bitcast.4) | data formatting | bytes 2949120
  93.9 1.3 %copy.16 = f32[1,2880]{1,0:T(1,128)} copy(f32[1,2880]{1,0:T(1,128)} %get-tuple-element.9) | data formatting | bytes 23040

commit v6 on v5

--- a/solution.py
+++ b/solution.py
@@ -214,10 +214,16 @@
 
     @pl.when(polar)
     def _():
-        for r in range(SPEC):
-            @pl.when(lon != owner(r))
+        def send_row(i, carry):
+            r = lax.rem(lon + i, SPEC)
+            slot, w = lax.div(r, nl), lax.rem(r, nl)
+            dev = lax.rem(w, 2) * half + lax.div(w, 2)
+
+            @pl.when(lon != dev)
             def _():
-                to_lon(a_ref.at[natural(r)], rowb.at[r // nl, lon], rows.at[0], rows.at[1 + r // nl], owner(r)).start()
+                to_lon(a_ref.at[natural(r)], rowb.at[slot, lon], rows.at[0], rows.at[1 + slot], dev).start()
+            return carry
+        lax.fori_loop(0, SPEC, send_row, 0)
 
     peers(lambda p: to_lon(seaw_ref.at[p], seab.at[pl.ds(rp * lon, rp)], seas.at[0], seas.at[1], p).start())
     lat_sends(coef_ref, coefr, csem)
@@ -564,15 +570,12 @@
                     twice[0] = (wave_ref[0] * add + 0.1 * near) * keept[...]
                     twice[1] = wave_ref[1] * swap(add, krow) * keept[...]
                 if t == STEPS - 1:
-                    for r in range(NPOLE):
-                        for dev in (r % half, half + r % half):
-                            @pl.when(lon != dev)
-                            def _():
-                                to_lon(sprev.at[r + 1], rs6.at[r // half, lon], r6.at[0], r6.at[1 + r // half], dev).start()
-
-                            @pl.when(lon == dev)
-                            def _():
-                                rs6[r // half, lon] = sprev[r + 1]
+                    def hand_on(dev):
+                        for slot in range(NPOLE // half):
+                            to_lon(sprev.at[slot * half + lax.rem(dev, half) + 1], rs6.at[slot, lon], r6.at[0], r6.at[1 + slot], dev).start()
+                    peers(hand_on)
+                    for slot in range(NPOLE // half):
+                        rs6[slot, lon] = sprev[slot * half + lax.rem(lon, half) + 1]
 
         around = (pltpu.roll(now, 1, 1) + pltpu.roll(now, LEV - 1, 1)
                   + sea[pl.ds(Q0 - 1, QN), :] + sea[pl.ds(Q0 + 1, QN), :])
@@ -670,11 +673,8 @@
             message_wait(ex, exs, t, 0)
         for t in range(1, STEPS):
             message_wait(fx, fxs, t, 0)
-        for r in range(NPOLE):
-            for dev in (r % half, half + r % half):
-                @pl.when(lon != dev)
-                def _():
-                    wait_bytes(sa.at[0], r6.at[0])
+        for slot in range(NPOLE // half):
+            peers(lambda p: wait_bytes(sa.at[0], r6.at[0]))
         for slot in range(NPOLE // half):
             wait_bytes(stage.at[slot, pl.ds(0, half - 1)], fsem.at[0])
 

time: 95.4 us -> 94.4 us (0.990)
  no operation moved by 1% of the time
where the time goes in v6:
time: 94.4 us; the launch traced here: 94.2 us
  Pallas kernels  89.7 us (95%)
  local copies, waits for them, and re-layouts  3.9 us (4%)
    pallas_call x1, Pallas kernels, local(): pl.pallas_call(functools.partial(kernel, nl), out_shape=(jax.ShapeDtypeSt...  89.7 us
    unnamed x2, local copies, waits for them, and re-layouts  3.9 us

profile of v6, /device:TPU:0, one launch (start us, length us, event | category | flops | bytes accessed | tf_op | source)
XLA Modules:
  0.0 94.2 jit_solution(7601139842667917754)
XLA Ops:
  0.6 89.7 %shard_map.122 = (f32[90,32,128]{2,1,0:T(8,128)}, f32[1,2880]{1,0:T(1,128)}) custom-call(f32[90,32,128]{2,1,0:T(8,128)} %bitcast.3, f32[1,2880]{1,0:T(1,128)} %sea_ref.1, s32[32,90]{1,0:T(8,128)} %land_ref.1, f32[1,128]{1,0:T(1,128)} %bitcast.5, f32[128,128]{1,0:T(8,128)} %vmix_ref.1, s32[32]{0:T(128)} %cut_ref.1, ...), custom_call_target="tpu_custom_call" | custom-call | tf_op jit(solution)/shard_map/pallas_call | solution.py:693
  90.3 2.6 %copy.15 = f32[32,90,128]{2,0,1:T(8,128)} copy(f32[32,90,128]{2,0,1:T(8,128)} %bitcast.4) | data formatting | bytes 2949120
  92.9 1.3 %copy.16 = f32[1,2880]{1,0:T(1,128)} copy(f32[1,2880]{1,0:T(1,128)} %get-tuple-element.9) | data formatting | bytes 23040
